TPU v7x, 128 devices: a whole 4x4x4 slice. The times are simulated.
128 devices in a mesh: fluid: 16 (over z, y), sub: 8 (over x, core).
Axes of the slice: x: 4, y: 4, z: 4, core: 2. Of those that a mesh axis runs over, the one named last changes fastest.
Arguments:
- positions: float32 [3, 262144], P(None, ('fluid', 'sub')), may hold values from 0 to 1
- particle_temp: float32 [262144], P(('fluid', 'sub')), may hold values from -6 to 6
- pair_list: int32 [32768, 2], P(('fluid', 'sub')), may hold values from 0 to 31, as said below
- pair_count: int32 [128], P(('fluid', 'sub')), may hold values from 16 to 256, as said below
- ghost_particle: int32 [262144], P(('fluid', 'sub')), may hold values from 0 to 2047
- ghost_owner: int32 [262144, 1], P(('fluid', 'sub')), may hold values from 0 to 127; in each aligned block of 2048 rows (0 to 2047, 2048 to 4095, ...) at most 32 rows name the same one
- ghost_cell: int32 [262144], P(('fluid', 'sub')), may hold values from 0 to 32767
- wall_seen: float32 [262144], P(('fluid', 'sub')), may hold values from -6 to 6
- solid_temp: float32 [32, 2048, 2048], P(None, ('fluid', 'sub')), may hold values from -6 to 6
- conduct: float32 [32, 2048, 2048], P(None, ('fluid', 'sub')), may hold values from 0.03 to 0.16
Outputs:
- particle_out: float32 [262144], P(('fluid', 'sub'))
- solid_out: float32 [32, 2048, 2048], P(None, ('fluid', 'sub'))
- ghost_temp: float32 [262144], P(('fluid', 'sub'))
Inputs may be any that keep to these rules, and one draw needn't show every extreme that they name: `pair_list`: column 0 names one of the device's own tiles; column 1 names own tile t below 16, or tile t - 16 of the next device along sub, cyclically. `pair_count`: rows of a device's block beyond its count are not used; some device uses all 256. `ghost_owner`: among the 2048 ghosts of one device, at most 32 name the same owner.
All inputs are finite; a program needn't handle non-finite values.
Results may differ from a plain program's by a relative error of at most 0.0003.
Values sent between devices are 32-bit elements; how exact they have to be, the bound alone decides.
A program may use at most 128 MiB of HBM per device.

v0:
```python
import jax
import jax.numpy as jnp
from jax import lax
from jax.sharding import PartitionSpec as P

TILE = 128
SUBSTEPS = 6


heat_rate = 0.004
wall_heat = 0.5


def from_behind(value, axis, by):
    length = lax.axis_size(axis)
    return lax.ppermute(value, axis, [(i, (i + by) % length) for i in range(length)])


def split_up(value, dim, length):
    before, after = (value.shape[:dim], value.shape[dim + 1 :])
    return jnp.moveaxis(value.reshape(*before, length, -1, *after), dim, 0)


def laid_out(pieces, dim):
    lengths = list(pieces.shape[1:])
    lengths[dim] *= pieces.shape[0]
    return jnp.moveaxis(pieces, 0, dim).reshape(lengths)


def exchange_both(value, axis, axes, splits, concats):
    sizes = [lax.axis_size(a) for a in axes]
    pieces = split_up(value, splits[0], sizes[0])
    pieces = jnp.moveaxis(split_up(pieces, splits[1] + 1, sizes[1]), 0, 1)
    inside = pieces.shape[2:]
    pieces = pieces.reshape(-1, *inside)
    pieces = lax.all_to_all(pieces, axis, split_axis=0, concat_axis=0, tiled=True)
    pieces = laid_out(pieces.reshape(*sizes, *inside), concats[0] + 1)
    return laid_out(pieces, concats[1])


def extended(value, sides, width):
    edges = {}
    for axis, dim in sides:
        size, length = (lax.axis_size(axis), value.shape[dim])
        up = [(i, (i + 1) % size) for i in range(size - 1)]
        last = lax.slice_in_dim(value, length - width, length, axis=dim)
        leading = lax.slice_in_dim(value, 0, width, axis=dim)
        edges[dim] = (
            lax.ppermute(last, axis, up),
            lax.ppermute(leading, axis, [(b, a) for a, b in up]),
        )
    done = []
    for _, dim in sides:
        low, high = edges[dim]
        around = [(width, width) if d in done else (0, 0) for d in range(value.ndim)]
        value = jnp.concatenate([jnp.pad(low, around), value, jnp.pad(high, around)], axis=dim)
        done.append(dim)
    return value


def tile_heat(own_pos, own_temp, near_pos, near_temp, pairs, live_count, blocks):
    all_pos = jnp.concatenate([own_pos, near_pos], axis=1)
    all_temp = jnp.concatenate([own_temp, near_temp], axis=0)
    block_rows = 16

    def pair_block(number, accrued):
        pair_rows = lax.dynamic_slice_in_dim(pairs, number * block_rows, block_rows, 0)
        first_tile = pair_rows[:, 0]
        second_tile = pair_rows[:, 1]
        live_rows = number * block_rows + jnp.arange(block_rows, dtype=jnp.int32) < live_count
        left_pos = all_pos[:, first_tile, :]
        right_pos = all_pos[:, second_tile, :]
        distance = jnp.zeros((block_rows, left_pos.shape[2], right_pos.shape[2]), jnp.float32)
        for component in range(3):
            offset = left_pos[component][:, :, None] - right_pos[component][:, None, :]
            distance = distance + offset * offset
        kernel = jnp.square(jnp.maximum(0.0, 1.0 - distance))
        gained = jnp.sum(
            kernel * (all_temp[second_tile][:, None, :] - all_temp[first_tile][:, :, None]), axis=2
        )
        gained = jnp.where(live_rows[:, None], gained, 0.0)
        return accrued.at[first_tile].add(gained)

    accrued = lax.fori_loop(0, blocks, pair_block, jnp.zeros(own_temp.shape, jnp.float32))
    return own_temp + heat_rate * accrued


def solid_step(padded, coef, source):
    center = padded[1:-1, 1:-1, 1:-1]
    beside = padded[2:, 1:-1, 1:-1] + padded[:-2, 1:-1, 1:-1]
    beside = beside + padded[1:-1, 2:, 1:-1] + padded[1:-1, :-2, 1:-1]
    beside = beside + padded[1:-1, 1:-1, 2:] + padded[1:-1, 1:-1, :-2]
    result = center + coef * (beside - 6.0 * center)
    return result.at[0].add(source)


def on_device(
    positions,
    particle_temp,
    pair_list,
    pair_count,
    ghost_particle,
    ghost_owner,
    ghost_cell,
    wall_seen,
    solid_temp,
    conduct,
):
    per_device = positions.shape[1]
    own_pos = positions.reshape(3, per_device // TILE, TILE)
    own_temp = particle_temp.reshape(per_device // TILE, TILE)
    near_pos, near_temp = from_behind((own_pos, own_temp), "sub", -1)
    live_count = pair_count[0]
    blocks = pair_list.shape[0] // 16
    heated = tile_heat(own_pos, own_temp, near_pos, near_temp, pair_list, live_count, blocks)
    particle_out = heated.reshape(-1)
    fluid_count = lax.axis_size("fluid")
    sub_count = lax.axis_size("sub")
    devices = fluid_count * sub_count
    ghosts = ghost_cell.shape[0]
    slots = max(2, 2 * ghosts // devices)
    owner = ghost_owner[:, 0]
    onehot = (owner[:, None] == jnp.arange(devices, dtype=jnp.int32)[None, :]).astype(jnp.int32)
    ranking = jnp.sum(jnp.cumsum(onehot, axis=0) * onehot, axis=1) - 1
    slot_index = owner * slots + ranking
    flux = wall_heat * (particle_out[ghost_particle] - wall_seen)
    send_flux = jnp.zeros((devices * slots,), jnp.float32).at[slot_index].set(flux)
    send_cell = (
        jnp.zeros((devices * slots,), jnp.float32)
        .at[slot_index]
        .set(ghost_cell.astype(jnp.float32))
    )
    recv_flux, recv_cell = (
        exchange_both(
            send_flux.reshape(fluid_count, sub_count, slots),
            ("fluid", "sub"),
            ("fluid", "sub"),
            (0, 1),
            (0, 1),
        ),
        exchange_both(
            send_cell.reshape(fluid_count, sub_count, slots),
            ("fluid", "sub"),
            ("fluid", "sub"),
            (0, 1),
            (0, 1),
        ),
    )
    recv_flux = recv_flux.reshape(-1)
    recv_cell = recv_cell.reshape(-1)
    cell_index = recv_cell.astype(jnp.int32)
    slab_width = solid_temp.shape[1]
    span_z = solid_temp.shape[2]
    surface = (
        jnp.zeros((slab_width * span_z,), jnp.float32)
        .at[cell_index]
        .add(recv_flux)
        .reshape(slab_width, span_z)
    )
    source = surface / SUBSTEPS
    temp = solid_temp
    for turn in range(SUBSTEPS):
        widened = extended(temp, ((("fluid", "sub"), 1),), 1)
        temp = solid_step(jnp.pad(widened, ((1, 1), (0, 0), (1, 1))), conduct, source)
    surface_now = temp[0].reshape(-1)[cell_index]
    returned = exchange_both(
        surface_now.reshape(fluid_count, sub_count, slots),
        ("fluid", "sub"),
        ("fluid", "sub"),
        (0, 1),
        (0, 1),
    ).reshape(-1)
    ghost_temp = returned[slot_index]
    return (particle_out, temp, ghost_temp)


def solution(mesh):
    placed = (
        P(None, ("fluid", "sub")),
        P(("fluid", "sub")),
        P(("fluid", "sub"), None),
        P(("fluid", "sub")),
        P(("fluid", "sub")),
        P(("fluid", "sub"), None),
        P(("fluid", "sub")),
        P(("fluid", "sub")),
        P(None, ("fluid", "sub"), None),
        P(None, ("fluid", "sub"), None),
    )
    return jax.shard_map(
        on_device,
        mesh=mesh,
        in_specs=placed,
        out_specs=(P(("fluid", "sub")), P(None, ("fluid", "sub"), None), P(("fluid", "sub"))),
        check_vma=False,
    )
```

profile of v0, /device:TPU:1, one launch (start us, length us, event | category | flops | bytes accessed | tf_op | source)
XLA Modules:
  0.0 458.6 jit_solution(9416736316855392495)
XLA Ops:
  7.3 8.1 %scatter_custom_fusion.1 = f32[4096]{0:T(1024)S(1)} fusion(s32[2048]{0:T(1024)S(1)} %bitcast.113, f32[2048]{0:T(1024)S(1)} %convert_element_type.38, f32[]{:T(128)} %constant.198.clone.1), kind=kCustom, calls=%fused_computation.133 | custom fusion | bytes 16388 | tf_op jit(solution)/shard_map/scatter | solution.py:131
  16.1 8.5 %all-to-all-start = ((f32[128,1,1,32]{3,2,1,0:T(1,128)}), f32[128,1,1,32]{3,2,1,0:T(1,128)S(1)}, u32[]{:S(2)}, u32[]{:S(2)}) async-start(f32[128,1,1,32]{3,2,1,0:T(1,128)} %bitcast.22), calls=%async_computation | async-start | bytes 131072 | tf_op jit(solution)/shard_map/all_to_all | solution.py:36
  24.6 4.6 %copy.42 = f32[32,16,2048]{2,0,1:T(8,128)S(1)} copy(f32[32,16,2048]{2,1,0:T(8,128)} %param.32) | data formatting | bytes 8388608 | tf_op args[8]
  37.1 86.8 %while.19 = (s32[]{:T(128)}, f32[16,128]{1,0:T(8,128)S(1)}, s32[256,2]{0,1:T(2,128)S(1)}, s32[]{:T(128)}, f32[3,32,128]{2,0,1:T(4,128)S(1)}, /*index=5*/f32[32,1...) while((s32[]{:T(128)}, f32[16,128]{1,0:T(8,128)S(1)}, ...), condition=%wide.region_3.4_spmd, body=%wide.region_0.3_spmd.sunk | while | flops 3674278 | bytes 329339 | solution.py:84
  123.9 11.8 %gather_fusion.4 = f32[2048]{0:T(1024)S(1)} fusion(f32[2048]{0:T(1024)S(1)} %add_bitcast_fusion, s32[2048]{0:T(1024)S(1)} %fusion.46), kind=kCustom, calls=%fused_computation.4 | custom fusion | bytes 24576 | tf_op jit(solution)/shard_map/gather | solution.py:126
  135.8 8.1 %scatter_custom_fusion.2 = f32[4096]{0:T(1024)S(1)} fusion(s32[2048]{0:T(1024)S(1)} %bitcast.114, f32[2048]{0:T(1024)S(1)} %subtract_multiply_fusion, f32[]{:T(128)} %constant.198.clone.1), kind=kCustom, calls=%fused_computation.131 | custom fusion | bytes 16388 | tf_op jit(solution)/shard_map/scatter | solution.py:127
  144.5 9.9 %all-to-all-start.1 = ((f32[128,1,1,32]{3,2,1,0:T(1,128)}), f32[128,1,1,32]{3,2,1,0:T(1,128)S(1)}, u32[]{:S(2)}, u32[]{:S(2)}) async-start(f32[128,1,1,32]{3,2,1,0:T(1,128)} %bitcast.28), calls=%async_computation.1 | async-start | bytes 131072 | tf_op jit(solution)/shard_map/all_to_all | solution.py:36
  154.4 9.6 %all-to-all-done.1 = f32[128,1,1,32]{3,2,1,0:T(1,128)S(1)} async-done(((f32[128,1,1,32]{3,2,1,0:T(1,128)}), f32[128,1,1,32]{3,2,1,0:T(1,128)S(1)}, u32[]{:S(2)}, u32[]{:S(2)}) %all-to-all-start.1) | async-done | bytes 16416 | tf_op jit(solution)/shard_map/all_to_all | solution.py:36
  164.1 24.7 %scatter_custom_fusion.3 = f32[32768]{0:T(1024)S(1)} fusion(s32[4096]{0:T(1024)S(1)} %bitcast.111, f32[4096]{0:T(1024)S(1)} %reshape.348, f32[]{:T(128)} %constant.198.clone.1), kind=kCustom, calls=%fused_computation.122 | custom fusion | flops 4096 | bytes 131076 | tf_op jit(solution)/shard_map/scatter-add | solution.py:157
  188.9 7.6 %select_maximum_fusion.10 = f32[34,18,2050]{2,0,1:T(8,128)S(1)} fusion(f32[32,1,2048]{2,0,1:T(8,128)S(1)} %collective-permute-done.3, f32[32,16,2048]{2,0,1:T(8,128)} %copy-done.7, f32[32,1,2048]{2,0,1:T(8,128)S(1)} %collective-permute-done.2), kind=kLoop, calls=%fused_computation.40 | loop fusion | flops 18819000 | bytes 9736992 | tf_op jit(solution)/shard_map/concatenate | solution.py:56
  196.4 10.4 %fusion.37 = f32[32,16,2048]{2,0,1:T(8,128)} fusion(f32[32,16,2048]{2,0,1:T(8,128)} %copy-done.7, f32[34,18,2050]{2,0,1:T(8,128)S(1)} %select_maximum_fusion.10, f32[32,1,2048]{2,0,1:T(8,128)S(1)} %collective-permute-done.2, f32[32,1,2048]{2,0,1:T(8,128)S(1)} %collective-permute-done.3, f32[32,16,2048]{2,1,0:T(8,128)S(1)} %copy-done.1), kind=kLoop, calls=%fused_computation.98 | loop fusion | flops 11534336 | bytes 29884416 | tf_op jit(solution)/shard_map/add | solution.py:93
  208.2 3.6 scatter-add.49
  219.2 4.7 %collective-permute-done.5 = f32[32,1,2048]{2,0,1:T(8,128)S(1)} collective-permute-done((f32[32,1,2048]{2,0,1:T(8,128)S(1)}, f32[32,1,2048]{2,0,1:T(8,128)S(1)}, u32[]{:S(2)}, u32[]{:S(2)}) %collective-permute-start.5) | collective-permute-done | bytes 262176 | tf_op jit(solution)/shard_map/ppermute | solution.py:50
  223.9 7.4 %select_maximum_fusion.8 = f32[34,18,2050]{2,0,1:T(8,128)S(1)} fusion(f32[32,1,2048]{2,0,1:T(8,128)S(1)} %collective-permute-done.5, f32[32,16,2048]{2,0,1:T(8,128)} %scatter-add.49, f32[32,1,2048]{2,0,1:T(8,128)S(1)} %collective-permute-done.4), kind=kLoop, calls=%fused_computation.38 | loop fusion | flops 18819000 | bytes 9736992 | tf_op jit(solution)/shard_map/concatenate | solution.py:56
  231.3 10.2 %fusion.32 = f32[32,16,2048]{2,0,1:T(8,128)} fusion(f32[32,16,2048]{2,0,1:T(8,128)} %scatter-add.49, f32[34,18,2050]{2,0,1:T(8,128)S(1)} %select_maximum_fusion.8, f32[32,1,2048]{2,0,1:T(8,128)S(1)} %collective-permute-done.4, f32[32,1,2048]{2,0,1:T(8,128)S(1)} %collective-permute-done.5, f32[32,16,2048]{2,1,0:T(8,128)S(1)} %copy-done.2), kind=kLoop, calls=%fused_computation.88 | loop fusion | flops 11534336 | bytes 29884416 | tf_op jit(solution)/shard_map/add | solution.py:93
  252.7 4.7 %collective-permute-done.7 = f32[32,1,2048]{2,0,1:T(8,128)S(1)} collective-permute-done((f32[32,1,2048]{2,0,1:T(8,128)S(1)}, f32[32,1,2048]{2,0,1:T(8,128)S(1)}, u32[]{:S(2)}, u32[]{:S(2)}) %collective-permute-start.7) | collective-permute-done | bytes 262176 | tf_op jit(solution)/shard_map/ppermute | solution.py:50
  257.4 7.4 %select_maximum_fusion.6 = f32[34,18,2050]{2,0,1:T(8,128)S(1)} fusion(f32[32,1,2048]{2,0,1:T(8,128)S(1)} %collective-permute-done.7, f32[32,16,2048]{2,0,1:T(8,128)} %scatter-add.50, f32[32,1,2048]{2,0,1:T(8,128)S(1)} %collective-permute-done.6), kind=kLoop, calls=%fused_computation.36 | loop fusion | flops 18819000 | bytes 9736992 | tf_op jit(solution)/shard_map/concatenate | solution.py:56
  264.8 10.4 %fusion.27 = f32[32,16,2048]{2,0,1:T(8,128)} fusion(f32[32,16,2048]{2,0,1:T(8,128)} %scatter-add.50, f32[34,18,2050]{2,0,1:T(8,128)S(1)} %select_maximum_fusion.6, f32[32,1,2048]{2,0,1:T(8,128)S(1)} %collective-permute-done.6, f32[32,1,2048]{2,0,1:T(8,128)S(1)} %collective-permute-done.7, f32[32,16,2048]{2,1,0:T(8,128)S(1)} %copy-done.3), kind=kLoop, calls=%fused_computation.78 | loop fusion | flops 11534336 | bytes 29884416 | tf_op jit(solution)/shard_map/add | solution.py:93
  276.6 3.6 scatter-add.51
  286.5 4.7 %collective-permute-done.9 = f32[32,1,2048]{2,0,1:T(8,128)S(1)} collective-permute-done((f32[32,1,2048]{2,0,1:T(8,128)S(1)}, f32[32,1,2048]{2,0,1:T(8,128)S(1)}, u32[]{:S(2)}, u32[]{:S(2)}) %collective-permute-start.9) | collective-permute-done | bytes 262176 | tf_op jit(solution)/shard_map/ppermute | solution.py:50
  291.2 7.4 %select_maximum_fusion.4 = f32[34,18,2050]{2,0,1:T(8,128)S(1)} fusion(f32[32,1,2048]{2,0,1:T(8,128)S(1)} %collective-permute-done.9, f32[32,16,2048]{2,0,1:T(8,128)} %scatter-add.51, f32[32,1,2048]{2,0,1:T(8,128)S(1)} %collective-permute-done.8), kind=kLoop, calls=%fused_computation.34 | loop fusion | flops 18819000 | bytes 9736992 | tf_op jit(solution)/shard_map/concatenate | solution.py:56
  298.6 10.2 %fusion.22 = f32[32,16,2048]{2,0,1:T(8,128)} fusion(f32[32,16,2048]{2,0,1:T(8,128)} %scatter-add.51, f32[34,18,2050]{2,0,1:T(8,128)S(1)} %select_maximum_fusion.4, f32[32,1,2048]{2,0,1:T(8,128)S(1)} %collective-permute-done.8, f32[32,1,2048]{2,0,1:T(8,128)S(1)} %collective-permute-done.9, f32[32,16,2048]{2,1,0:T(8,128)S(1)} %copy-done.4), kind=kLoop, calls=%fused_computation.68 | loop fusion | flops 11534336 | bytes 29884416 | tf_op jit(solution)/shard_map/add | solution.py:93
  320.0 4.7 %collective-permute-done.11 = f32[32,1,2048]{2,0,1:T(8,128)S(1)} collective-permute-done((f32[32,1,2048]{2,0,1:T(8,128)S(1)}, f32[32,1,2048]{2,0,1:T(8,128)S(1)}, u32[]{:S(2)}, u32[]{:S(2)}) %collective-permute-start.11) | collective-permute-done | bytes 262176 | tf_op jit(solution)/shard_map/ppermute | solution.py:50
  324.8 7.4 %select_maximum_fusion.2 = f32[34,18,2050]{2,0,1:T(8,128)S(1)} fusion(f32[32,1,2048]{2,0,1:T(8,128)S(1)} %collective-permute-done.11, f32[32,16,2048]{2,0,1:T(8,128)} %scatter-add.52, f32[32,1,2048]{2,0,1:T(8,128)S(1)} %collective-permute-done.10), kind=kLoop, calls=%fused_computation.32 | loop fusion | flops 18819000 | bytes 9736992 | tf_op jit(solution)/shard_map/concatenate | solution.py:56
  332.2 10.4 %fusion.17 = f32[32,16,2048]{2,0,1:T(8,128)} fusion(f32[32,16,2048]{2,0,1:T(8,128)} %scatter-add.52, f32[34,18,2050]{2,0,1:T(8,128)S(1)} %select_maximum_fusion.2, f32[32,1,2048]{2,0,1:T(8,128)S(1)} %collective-permute-done.10, f32[32,1,2048]{2,0,1:T(8,128)S(1)} %collective-permute-done.11, f32[32,16,2048]{2,1,0:T(8,128)S(1)} %copy-done.5), kind=kLoop, calls=%fused_computation.58 | loop fusion | flops 11534336 | bytes 29884416 | tf_op jit(solution)/shard_map/add | solution.py:93
  353.8 6.5 %collective-permute-done.13 = f32[32,1,2048]{2,0,1:T(8,128)S(1)} collective-permute-done((f32[32,1,2048]{2,0,1:T(8,128)S(1)}, f32[32,1,2048]{2,0,1:T(8,128)S(1)}, u32[]{:S(2)}, u32[]{:S(2)}) %collective-permute-start.13) | collective-permute-done | bytes 262176 | tf_op jit(solution)/shard_map/ppermute | solution.py:50
  360.3 7.4 %select_maximum_fusion = f32[34,18,2050]{2,0,1:T(8,128)S(1)} fusion(f32[32,1,2048]{2,0,1:T(8,128)S(1)} %collective-permute-done.13, f32[32,16,2048]{2,0,1:T(8,128)} %scatter-add.53, f32[32,1,2048]{2,0,1:T(8,128)S(1)} %collective-permute-done.12), kind=kLoop, calls=%fused_computation.30 | loop fusion | flops 18819000 | bytes 9736992 | tf_op jit(solution)/shard_map/concatenate | solution.py:56
  367.8 10.2 %fusion.12 = f32[32,16,2048]{2,0,1:T(8,128)} fusion(f32[32,16,2048]{2,0,1:T(8,128)} %scatter-add.53, f32[34,18,2050]{2,0,1:T(8,128)S(1)} %select_maximum_fusion, f32[32,1,2048]{2,0,1:T(8,128)S(1)} %collective-permute-done.12, f32[32,1,2048]{2,0,1:T(8,128)S(1)} %collective-permute-done.13, f32[32,16,2048]{2,1,0:T(8,128)S(1)} %copy-done.6), kind=kLoop, calls=%fused_computation.48 | loop fusion | flops 11534336 | bytes 29884416 | tf_op jit(solution)/shard_map/add | solution.py:93
  379.3 23.0 %gather_fusion.5 = f32[4096]{0:T(1024)S(1)} fusion(f32[32768]{0:T(1024)S(1)} %bitcast.91, s32[4096]{0:T(1024)S(1)} %broadcast_clamp_fusion), kind=kCustom, calls=%fused_computation.5 | custom fusion | bytes 49152 | tf_op jit(solution)/shard_map/gather | solution.py:165
  403.1 24.4 %all-to-all-start.2 = ((f32[128,1,1,32]{3,2,1,0:T(1,128)}), f32[128,1,1,32]{3,2,1,0:T(1,128)S(1)}, u32[]{:S(2)}, u32[]{:S(2)}) async-start(f32[128,1,1,32]{3,2,1,0:T(1,128)} %bitcast.35), calls=%async_computation.2 | async-start | bytes 131072 | tf_op jit(solution)/shard_map/all_to_all | solution.py:36
  431.1 6.6 %copy.53 = f32[32,16,2048]{2,1,0:T(8,128)} copy(f32[32,16,2048]{2,0,1:T(8,128)} %scatter-add.54) | data formatting | bytes 8388608
  437.8 20.5 %gather_fusion.6 = f32[2048]{0:T(1024)} fusion(f32[4096]{0:T(1024)S(1)} %reshape_reshape.8, s32[2048]{0:T(1024)S(1)} %broadcast_clamp_fusion.1), kind=kCustom, calls=%fused_computation.6 | custom fusion | bytes 24576 | tf_op jit(solution)/shard_map/gather | solution.py:173
  (289 shorter events, 157.5 us)
Async XLA Ops:
  0.6 6.0 %copy-start.8 = (s32[2048,1]{0,1:T(1,128)S(1)}, s32[2048,1]{0,1:T(1,128)}, u32[]{:S(2)}) copy-start(s32[2048,1]{0,1:T(1,128)} %param.29) | copy-start | bytes 24580
  0.6 36.2 %collective-permute-start.1 = (f32[16,128]{1,0:T(8,128)}, f32[16,128]{1,0:T(8,128)S(1)}, u32[]{:S(2)}, u32[]{:S(2)}) collective-permute-start(f32[16,128]{1,0:T(8,128)} %bitcast.117), channel_id=1, source_target_pairs={{0,7},{1,0},{2,1},{3,2},{4,3},{5,4},{6,5},{7,6},{8,15},{9,8},{10,9... | collective-permute-start | bytes 24584 | tf_op jit(solution)/shard_map/ppermute | solution.py:16
  2.0 35.0 %collective-permute-start = (f32[3,16,128]{2,0,1:T(4,128)}, f32[3,16,128]{2,0,1:T(4,128)S(1)}, u32[]{:S(2)}, u32[]{:S(2)}) collective-permute-start(f32[3,16,128]{2,0,1:T(4,128)} %bitcast.119), channel_id=1, source_target_pairs={{0,7},{1,0},{2,1},{3,2},{4,3},{5,4},{6,5},{7,6},{8,15},{9,8},{10,9... | collective-permute-start | bytes 73736 | tf_op jit(solution)/shard_map/ppermute | solution.py:16
  16.1 20.8 %all-to-all-start = ((f32[128,1,1,32]{3,2,1,0:T(1,128)}), f32[128,1,1,32]{3,2,1,0:T(1,128)S(1)}, u32[]{:S(2)}, u32[]{:S(2)}) async-start(f32[128,1,1,32]{3,2,1,0:T(1,128)} %bitcast.22), calls=%async_computation | async-start | bytes 131072 | tf_op jit(solution)/shard_map/all_to_all | solution.py:36
  24.6 12.2 %copy-start.13 = (s32[2048]{0:T(1024)S(1)}, s32[2048]{0:T(1024)}, u32[]{:S(2)}) copy-start(s32[2048]{0:T(1024)} %param.28) | copy-start | bytes 24580
  24.6 12.2 %copy-start.9 = (f32[2048]{0:T(1024)S(1)}, f32[2048]{0:T(1024)}, u32[]{:S(2)}) copy-start(f32[2048]{0:T(1024)} %param.25) | copy-start | bytes 24580
  24.6 12.4 %copy-start.10 = (f32[3,2048]{1,0:T(4,128)S(1)}, f32[3,2048]{1,0:T(4,128)}, u32[]{:S(2)}) copy-start(f32[3,2048]{1,0:T(4,128)} %param.24) | copy-start | bytes 73732
  24.6 12.5 %copy-start.11 = (s32[256,2]{0,1:T(2,128)S(1)}, s32[256,2]{0,1:T(2,128)}, u32[]{:S(2)}) copy-start(s32[256,2]{0,1:T(2,128)} %param.26) | copy-start | bytes 6148
  29.3 2.0 copy-start.7
  31.3 157.5 %collective-permute-start.2 = (f32[32,1,2048]{2,0,1:T(8,128)S(1)}, f32[32,1,2048]{2,0,1:T(8,128)S(1)}, u32[]{:S(2)}, u32[]{:S(2)}) collective-permute-start(f32[32,1,2048]{2,0,1:T(8,128)S(1)} %get-tuple-element.224), channel_id=1, source_target_pairs={{0,1},{1,2},{2,3},{3,4},{4,5},{5,6},{6,7},{7,8},{8,9},{9,10},{10,1... | collective-permute-start | bytes 786440 | tf_op jit(solution)/shard_map/ppermute | solution.py:49
  34.9 154.0 %collective-permute-start.3 = (f32[32,1,2048]{2,0,1:T(8,128)S(1)}, f32[32,1,2048]{2,0,1:T(8,128)S(1)}, u32[]{:S(2)}, u32[]{:S(2)}) collective-permute-start(f32[32,1,2048]{2,0,1:T(8,128)S(1)} %get-tuple-element.225), channel_id=1, source_target_pairs={{1,0},{2,1},{3,2},{4,3},{5,4},{6,5},{7,6},{8,7},{9,8},{10,9},{11,1... | collective-permute-start | bytes 786440 | tf_op jit(solution)/shard_map/ppermute | solution.py:50
  123.9 11.8 %copy-start = (f32[2048]{0:T(1024)}, f32[2048]{0:T(1024)S(1)}, u32[]{:S(2)}) copy-start(f32[2048]{0:T(1024)S(1)} %add_bitcast_fusion) | copy-start | bytes 24580
  123.9 11.8 %copy-start.12 = (f32[2048]{0:T(1024)S(1)}, f32[2048]{0:T(1024)}, u32[]{:S(2)}) copy-start(f32[2048]{0:T(1024)} %param.31) | copy-start | bytes 24580
  144.5 19.5 %all-to-all-start.1 = ((f32[128,1,1,32]{3,2,1,0:T(1,128)}), f32[128,1,1,32]{3,2,1,0:T(1,128)S(1)}, u32[]{:S(2)}, u32[]{:S(2)}) async-start(f32[128,1,1,32]{3,2,1,0:T(1,128)} %bitcast.28), calls=%async_computation.1 | async-start | bytes 131072 | tf_op jit(solution)/shard_map/all_to_all | solution.py:36
  188.8 7.6 %copy-start.1 = (f32[32,16,2048]{2,1,0:T(8,128)S(1)}, f32[32,16,2048]{2,1,0:T(8,128)}, u32[]{:S(2)}) copy-start(f32[32,16,2048]{2,1,0:T(8,128)} %param.33) | copy-start | bytes 12582916
  212.9 6.3 %collective-permute-start.4 = (f32[32,1,2048]{2,0,1:T(8,128)S(1)}, f32[32,1,2048]{2,0,1:T(8,128)S(1)}, u32[]{:S(2)}, u32[]{:S(2)}) collective-permute-start(f32[32,1,2048]{2,0,1:T(8,128)S(1)} %get-tuple-element.222), channel_id=1, source_target_pairs={{0,1},{1,2},{2,3},{3,4},{4,5},{5,6},{6,7},{7,8},{8,9},{9,10},{10,1... | collective-permute-start | bytes 786440 | tf_op jit(solution)/shard_map/ppermute | solution.py:49
  215.9 15.4 %copy-start.2 = (f32[32,16,2048]{2,1,0:T(8,128)S(1)}, f32[32,16,2048]{2,1,0:T(8,128)}, u32[]{:S(2)}) copy-start(f32[32,16,2048]{2,1,0:T(8,128)} %param.33) | copy-start | bytes 12582916
  215.9 8.0 %collective-permute-start.5 = (f32[32,1,2048]{2,0,1:T(8,128)S(1)}, f32[32,1,2048]{2,0,1:T(8,128)S(1)}, u32[]{:S(2)}, u32[]{:S(2)}) collective-permute-start(f32[32,1,2048]{2,0,1:T(8,128)S(1)} %get-tuple-element.223), channel_id=1, source_target_pairs={{1,0},{2,1},{3,2},{4,3},{5,4},{6,5},{7,6},{8,7},{9,8},{10,9},{11,1... | collective-permute-start | bytes 786440 | tf_op jit(solution)/shard_map/ppermute | solution.py:50
  247.5 5.2 %collective-permute-start.6 = (f32[32,1,2048]{2,0,1:T(8,128)S(1)}, f32[32,1,2048]{2,0,1:T(8,128)S(1)}, u32[]{:S(2)}, u32[]{:S(2)}) collective-permute-start(f32[32,1,2048]{2,0,1:T(8,128)S(1)} %get-tuple-element.220), channel_id=1, source_target_pairs={{0,1},{1,2},{2,3},{3,4},{4,5},{5,6},{6,7},{7,8},{8,9},{9,10},{10,1... | collective-permute-start | bytes 786440 | tf_op jit(solution)/shard_map/ppermute | solution.py:49
  249.4 15.4 %copy-start.3 = (f32[32,16,2048]{2,1,0:T(8,128)S(1)}, f32[32,16,2048]{2,1,0:T(8,128)}, u32[]{:S(2)}) copy-start(f32[32,16,2048]{2,1,0:T(8,128)} %param.33) | copy-start | bytes 12582916
  249.4 8.0 %collective-permute-start.7 = (f32[32,1,2048]{2,0,1:T(8,128)S(1)}, f32[32,1,2048]{2,0,1:T(8,128)S(1)}, u32[]{:S(2)}, u32[]{:S(2)}) collective-permute-start(f32[32,1,2048]{2,0,1:T(8,128)S(1)} %get-tuple-element.221), channel_id=1, source_target_pairs={{1,0},{2,1},{3,2},{4,3},{5,4},{6,5},{7,6},{8,7},{9,8},{10,9},{11,1... | collective-permute-start | bytes 786440 | tf_op jit(solution)/shard_map/ppermute | solution.py:50
  281.3 5.2 %collective-permute-start.8 = (f32[32,1,2048]{2,0,1:T(8,128)S(1)}, f32[32,1,2048]{2,0,1:T(8,128)S(1)}, u32[]{:S(2)}, u32[]{:S(2)}) collective-permute-start(f32[32,1,2048]{2,0,1:T(8,128)S(1)} %get-tuple-element.218), channel_id=1, source_target_pairs={{0,1},{1,2},{2,3},{3,4},{4,5},{5,6},{6,7},{7,8},{8,9},{9,10},{10,1... | collective-permute-start | bytes 786440 | tf_op jit(solution)/shard_map/ppermute | solution.py:49
  283.2 15.4 %copy-start.4 = (f32[32,16,2048]{2,1,0:T(8,128)S(1)}, f32[32,16,2048]{2,1,0:T(8,128)}, u32[]{:S(2)}) copy-start(f32[32,16,2048]{2,1,0:T(8,128)} %param.33) | copy-start | bytes 12582916
  283.2 8.0 %collective-permute-start.9 = (f32[32,1,2048]{2,0,1:T(8,128)S(1)}, f32[32,1,2048]{2,0,1:T(8,128)S(1)}, u32[]{:S(2)}, u32[]{:S(2)}) collective-permute-start(f32[32,1,2048]{2,0,1:T(8,128)S(1)} %get-tuple-element.219), channel_id=1, source_target_pairs={{1,0},{2,1},{3,2},{4,3},{5,4},{6,5},{7,6},{8,7},{9,8},{10,9},{11,1... | collective-permute-start | bytes 786440 | tf_op jit(solution)/shard_map/ppermute | solution.py:50
  314.8 5.2 %collective-permute-start.10 = (f32[32,1,2048]{2,0,1:T(8,128)S(1)}, f32[32,1,2048]{2,0,1:T(8,128)S(1)}, u32[]{:S(2)}, u32[]{:S(2)}) collective-permute-start(f32[32,1,2048]{2,0,1:T(8,128)S(1)} %get-tuple-element.216), channel_id=1, source_target_pairs={{0,1},{1,2},{2,3},{3,4},{4,5},{5,6},{6,7},{7,8},{8,9},{9,10},{10,1... | collective-permute-start | bytes 786440 | tf_op jit(solution)/shard_map/ppermute | solution.py:49
  316.7 15.4 %copy-start.5 = (f32[32,16,2048]{2,1,0:T(8,128)S(1)}, f32[32,16,2048]{2,1,0:T(8,128)}, u32[]{:S(2)}) copy-start(f32[32,16,2048]{2,1,0:T(8,128)} %param.33) | copy-start | bytes 12582916
  316.7 8.0 %collective-permute-start.11 = (f32[32,1,2048]{2,0,1:T(8,128)S(1)}, f32[32,1,2048]{2,0,1:T(8,128)S(1)}, u32[]{:S(2)}, u32[]{:S(2)}) collective-permute-start(f32[32,1,2048]{2,0,1:T(8,128)S(1)} %get-tuple-element.217), channel_id=1, source_target_pairs={{1,0},{2,1},{3,2},{4,3},{5,4},{6,5},{7,6},{8,7},{9,8},{10,9},{11,1... | collective-permute-start | bytes 786440 | tf_op jit(solution)/shard_map/ppermute | solution.py:50
  348.6 5.2 %collective-permute-start.12 = (f32[32,1,2048]{2,0,1:T(8,128)S(1)}, f32[32,1,2048]{2,0,1:T(8,128)S(1)}, u32[]{:S(2)}, u32[]{:S(2)}) collective-permute-start(f32[32,1,2048]{2,0,1:T(8,128)S(1)} %get-tuple-element.214), channel_id=1, source_target_pairs={{0,1},{1,2},{2,3},{3,4},{4,5},{5,6},{6,7},{7,8},{8,9},{9,10},{10,1... | collective-permute-start | bytes 786440 | tf_op jit(solution)/shard_map/ppermute | solution.py:49
  350.5 9.8 %collective-permute-start.13 = (f32[32,1,2048]{2,0,1:T(8,128)S(1)}, f32[32,1,2048]{2,0,1:T(8,128)S(1)}, u32[]{:S(2)}, u32[]{:S(2)}) collective-permute-start(f32[32,1,2048]{2,0,1:T(8,128)S(1)} %get-tuple-element.215), channel_id=1, source_target_pairs={{1,0},{2,1},{3,2},{4,3},{5,4},{6,5},{7,6},{8,7},{9,8},{10,9},{11,1... | collective-permute-start | bytes 786440 | tf_op jit(solution)/shard_map/ppermute | solution.py:50
  353.2 14.6 %copy-start.6 = (f32[32,16,2048]{2,1,0:T(8,128)S(1)}, f32[32,16,2048]{2,1,0:T(8,128)}, u32[]{:S(2)}) copy-start(f32[32,16,2048]{2,1,0:T(8,128)} %param.33) | copy-start | bytes 12582916
  403.1 34.7 %all-to-all-start.2 = ((f32[128,1,1,32]{3,2,1,0:T(1,128)}), f32[128,1,1,32]{3,2,1,0:T(1,128)S(1)}, u32[]{:S(2)}, u32[]{:S(2)}) async-start(f32[128,1,1,32]{3,2,1,0:T(1,128)} %bitcast.35), calls=%async_computation.2 | async-start | bytes 131072 | tf_op jit(solution)/shard_map/all_to_all | solution.py:36
where the time goes:
time: 468 us; the launch traced here: 459 us
  other arithmetic  189 us (40%)
  local copies, waits for them, and re-layouts  154 us (33%)
  starting transfers between devices  76.7 us (16%)
  waiting for transfers between devices  37.1 us (8%)
    add x6, other arithmetic, solid_step(): result = center + coef * (beside - 6.0 * center)  61.8 us
    concatenate x6, other arithmetic, extended(): jnp.concatenate([jnp.pad(low, around), value, jnp.pad(high, around)], axi...  44.6 us
    all_to_all x3, starting transfers between devices, exchange_both(): lax.all_to_all(pieces, axis, split_axis=0, concat_axis=0, tiled=True)  42.8 us
    ppermute x6, waiting for transfers between devices, extended(): lax.ppermute(leading, axis, [(b, a) for a, b in up])  25.3 us
    reduce_sum x16, other arithmetic, pair_block(): jnp.sum(kernel * (all_temp[second_tile][:, None, :] - all_temp[first_tile...  25.2 us
    scatter-add x1, other arithmetic, on_device(): surface = jnp.zeros((slab_width * span_z,), jnp.float32).at[cell_index].a...  24.7 us
    gather x1, local copies, waits for them, and re-layouts, on_device(): surface_now = temp[0].reshape(-1)[cell_index]  23 us
    scatter-add x6, local copies, waits for them, and re-layouts, solid_step(): return result.at[0].add(source)  21.4 us
  transfers between devices with their start and end apart: 17, of which 11 were waited for; matrix products, arithmetic and copies ran while one was open for 34% of the time, Pallas kernels for 0%

commit v1 on v0

v1 whole, which is shorter than its diff:
```python
import functools
import jax
import jax.numpy as jnp
from jax import lax
from jax.experimental import pallas as pl
from jax.experimental.pallas import tpu as pltpu
from jax.sharding import PartitionSpec as P

F32, BF16, I32 = jnp.float32, jnp.bfloat16, jnp.int32
TILE = 128
SUBSTEPS = 6
SLOTS = 32
HEAT_RATE = 0.004
WALL_HEAT = 0.5
UNROLL = 8
AXES = ("fluid", "sub")
VMEM_SPEC = pl.BlockSpec(memory_space=pltpu.VMEM)
SMEM_SPEC = pl.BlockSpec(memory_space=pltpu.SMEM)
ANY_SPEC = pl.BlockSpec(memory_space=pl.ANY)


def split3(x):
    high = x.astype(BF16).astype(F32)
    rest = x - high
    mid = rest.astype(BF16).astype(F32)
    return high, mid, rest - mid


def row_of(ref):
    return jnp.concatenate([ref[t : t + 1, :] for t in range(ref.shape[0])], axis=1)


def onehot(rows, codes, dtype=BF16):
    shape = (rows, codes.shape[1])
    hit = lax.broadcasted_iota(I32, shape, 0) == jnp.broadcast_to(codes, shape)
    return jnp.where(hit, 1.0, 0.0).astype(dtype)


def dot_nn(a, b):
    return lax.dot_general(a, b, (((1,), (0,)), ((), ())), preferred_element_type=F32)


def dot_nt(a, b):
    return lax.dot_general(a, b, (((1,), (1,)), ((), ())), preferred_element_type=F32)


def put_features(pos, temp_row, left, right):
    wide = pos.shape[1]
    moved = pos - 0.5
    high, mid, low = split3(moved)
    squares = jnp.sum(moved * moved, axis=0, keepdims=True)
    one = jnp.ones((3, wide), F32)
    minus = split3(-squares)
    temps = split3(temp_row)
    for place, part in enumerate((high, high, mid, mid, high, low)):
        left[3 * place : 3 * place + 3, :] = part
    left[18:21, :] = one
    for k in range(3):
        left[21 + k : 22 + k, :] = minus[k]
        left[24 + k : 25 + k, :] = temps[k]
    left[27:30, :] = one
    left[30:32, :] = jnp.zeros((2, wide), F32)
    if right is None:
        return
    base = split3(1.0 - squares)
    for place, part in enumerate((high, mid, high, mid, low, high)):
        right[3 * place : 3 * place + 3, :] = 2.0 * part
    right[21:24, :] = one
    right[24:27, :] = one
    for k in range(3):
        right[18 + k : 19 + k, :] = base[k]
        right[27 + k : 28 + k, :] = -temps[k]
    right[30:32, :] = jnp.zeros((2, wide), F32)


def pair_heat(own_pos, own_temp, near_pos, near_temp, codes, count, left, right, lefts, rights, acc):
    tiles = own_temp.shape[0]
    for base, pos, temp, second in ((0, own_pos, own_temp, right), (tiles, near_pos, near_temp, None)):
        put_features(pos[...], row_of(temp), left, second)
        for t in range(tiles):
            block = left[:, t * TILE : (t + 1) * TILE]
            lefts[base + t] = block.T.astype(BF16)
    for t in range(tiles):
        block = right[:, t * TILE : (t + 1) * TILE]
        upper = lax.broadcasted_iota(I32, block.shape, 0) < 24
        rights[t, :, 0:TILE] = jnp.where(upper, block, 0.0).astype(BF16)
        rights[t, :, TILE : 2 * TILE] = jnp.where(upper, 0.0, block).astype(BF16)
    acc[...] = jnp.zeros(acc.shape, F32)
    live = count[0]

    def body(group, _):
        for k in range(UNROLL):
            number = group * UNROLL + k
            code = codes[number]
            first = lax.shift_right_logical(code, 5) & (tiles - 1)
            second = code & (2 * tiles - 1)
            both = dot_nn(lefts[second], rights[first])
            near = jnp.maximum(both[:, :TILE], 0.0)
            gained = near * near * both[:, TILE:]
            gained = jnp.sum(gained.reshape(TILE // 8, 8, TILE), axis=0)
            acc[first] += jnp.where(number < live, gained, 0.0)
        return 0

    lax.fori_loop(0, (live + UNROLL - 1) // UNROLL, body, 0)
    return own_temp[...] + HEAT_RATE * jnp.sum(acc[...], axis=1)


def ranks(owners, devices):
    row = lax.broadcasted_iota(I32, (TILE, 2 * TILE), 0)
    col = lax.broadcasted_iota(I32, (TILE, 2 * TILE), 1)
    before = jnp.where((row < col) | (col >= TILE), 1.0, 0.0).astype(BF16)
    so_far = jnp.zeros((devices, TILE), F32)
    out = []
    for t in range(owners.shape[1] // TILE):
        mine = owners[:, t * TILE : (t + 1) * TILE]
        counted = dot_nn(mine, before)
        out.append(jnp.sum(mine.astype(F32) * (counted[:, :TILE] + so_far), axis=0, keepdims=True))
        so_far = so_far + counted[:, TILE:]
    return jnp.concatenate(out, axis=1)


def particles_kernel(codes, count, own_pos, own_temp, near_pos, near_temp, which, owner, cell, seen,
                     heated, send, rank_out, left, right, lefts, rights, acc):
    out = pair_heat(own_pos, own_temp, near_pos, near_temp, codes, count, left, right, lefts, rights, acc)
    heated[...] = out
    devices = send.shape[0]
    owners = onehot(devices, row_of(owner))
    rank = ranks(owners, devices)
    for t in range(rank_out.shape[0]):
        rank_out[t : t + 1, :] = rank[:, t * TILE : (t + 1) * TILE].astype(I32)
    tiles = out.shape[0]
    parts = jnp.concatenate(split3(out), axis=0).T.astype(BF16)
    which_row = row_of(which)
    high = onehot(tiles, lax.shift_right_logical(which_row, 7))
    picked = dot_nn(parts, jnp.concatenate([high] * 3, axis=0))
    low = jnp.broadcast_to(which_row & (TILE - 1), picked.shape)
    hit = lax.broadcasted_iota(I32, picked.shape, 0) == low
    value = jnp.sum(jnp.where(hit, picked, 0.0), axis=0, keepdims=True)
    flux = WALL_HEAT * (value - row_of(seen))
    slot = onehot(SLOTS, rank.astype(I32), F32)
    cell_row = row_of(cell)
    cell_high = (cell_row & ~255).astype(F32)
    cell_low = (cell_row & 255).astype(F32)
    fluxes = split3(flux)
    total = jnp.zeros((devices, 2 * SLOTS), F32)
    for f, c in zip(fluxes, (cell_high, cell_low, jnp.zeros_like(cell_low))):
        rows = jnp.concatenate([slot * f, slot * c], axis=0).astype(BF16)
        total = total + dot_nt(owners, rows)
    send[...] = jnp.zeros(send.shape, F32)
    send[:, 0 : 2 * SLOTS] = total


def call_particles(codes, count, own_pos, own_temp, near_pos, near_temp, which, owner, cell, seen, devices):
    tiles = own_temp.shape[0]
    wide = own_pos.shape[1]
    return pl.pallas_call(
        particles_kernel,
        out_shape=(
            jax.ShapeDtypeStruct(own_temp.shape, F32),
            jax.ShapeDtypeStruct((devices, TILE), F32),
            jax.ShapeDtypeStruct(owner.shape, I32),
        ),
        in_specs=[SMEM_SPEC] * 2 + [VMEM_SPEC] * 8,
        out_specs=(VMEM_SPEC,) * 3,
        scratch_shapes=[
            pltpu.VMEM((32, wide), F32),
            pltpu.VMEM((32, wide), F32),
            pltpu.VMEM((2 * tiles, TILE, 32), BF16),
            pltpu.VMEM((tiles, 32, 2 * TILE), BF16),
            pltpu.VMEM((tiles, 8, TILE), F32),
        ],
        name="particles",
    )(codes, count, own_pos, own_temp, near_pos, near_temp, which, owner, cell, seen)


def spread_kernel(recv, surface, hot, lows):
    turned = recv[...].T
    slots, sources = SLOTS, recv.shape[0]
    for s in range(slots):
        code = turned[slots + s : slots + s + 1, :].astype(I32)
        flux = turned[s : s + 1, :]
        at = pl.ds(s * sources, sources)
        hot[:, at] = onehot(hot.shape[0], lax.shift_right_logical(code, 7))
        low = onehot(TILE, code & (TILE - 1), F32)
        for k, part in enumerate(split3(flux)):
            lows[k, :, at] = (low * part).astype(BF16)
    total = dot_nt(hot[...], lows[0])
    total = total + dot_nt(hot[...], lows[1])
    surface[...] = total + dot_nt(hot[...], lows[2])


def call_spread(recv, cells):
    rows = cells // TILE
    slots = recv.shape[0] * SLOTS
    return pl.pallas_call(
        spread_kernel,
        out_shape=jax.ShapeDtypeStruct((rows, TILE), F32),
        in_specs=[VMEM_SPEC],
        out_specs=VMEM_SPEC,
        scratch_shapes=[pltpu.VMEM((rows, slots), BF16), pltpu.VMEM((3, TILE, slots), BF16)],
        name="spread",
    )(recv)


def pick_kernel(surface, recv, values):
    turned = recv[...].T
    rows = surface.shape[0]
    flat = surface[...]
    parts = [p.astype(BF16) for p in split3(jnp.concatenate([flat[k : k + TILE, :].T for k in range(0, rows, TILE)], axis=1))]
    sources = recv.shape[0]
    out = []
    for s in range(SLOTS):
        code = turned[SLOTS + s : SLOTS + s + 1, :].astype(I32)
        high = onehot(rows, lax.shift_right_logical(code, 7))
        found = dot_nn(parts[0], high) + dot_nn(parts[1], high) + dot_nn(parts[2], high)
        low = lax.broadcasted_iota(I32, found.shape, 0) == jnp.broadcast_to(code & (TILE - 1), found.shape)
        out.append(jnp.sum(jnp.where(low, found, 0.0), axis=0, keepdims=True))
    out.append(jnp.zeros((TILE - SLOTS, sources), F32))
    values[...] = jnp.concatenate(out, axis=0).T


def call_pick(surface, recv):
    return pl.pallas_call(
        pick_kernel,
        out_shape=jax.ShapeDtypeStruct(recv.shape, F32),
        in_specs=[VMEM_SPEC] * 2,
        out_specs=VMEM_SPEC,
        name="pick",
    )(surface, recv)


def unpack_kernel(values, owner, rank, out):
    devices = values.shape[0]
    owners = onehot(devices, row_of(owner))
    turned = values[...].T[0:SLOTS, :]
    parts = jnp.concatenate(split3(turned), axis=0).astype(BF16)
    found = dot_nn(parts, owners)
    slot = onehot(SLOTS, row_of(rank), F32)
    total = found[0:SLOTS] + found[SLOTS : 2 * SLOTS] + found[2 * SLOTS :]
    ghost = jnp.sum(total * slot, axis=0, keepdims=True)
    for t in range(out.shape[0]):
        out[t : t + 1, :] = ghost[:, t * TILE : (t + 1) * TILE]


def call_unpack(values, owner, rank):
    return pl.pallas_call(
        unpack_kernel,
        out_shape=jax.ShapeDtypeStruct(owner.shape, F32),
        in_specs=[VMEM_SPEC] * 3,
        out_specs=VMEM_SPEC,
        name="unpack",
    )(values, owner, rank)


MESH = pl.DeviceIdType.MESH


def where_is(index, subs):
    return (index // subs, index % subs)


def exchange_kernel(devices, subs, send, recv, send_sem, recv_sem, own_sem):
    me = lax.axis_index(AXES[0]) * subs + lax.axis_index(AXES[1])
    barrier = pltpu.get_barrier_semaphore()

    def greet(k, _):
        to = lax.rem(me + k, devices)
        pl.semaphore_signal(barrier, inc=1, device_id=where_is(to, subs), device_id_type=MESH)
        return 0

    lax.fori_loop(1, devices, greet, 0)
    own = pltpu.make_async_copy(send.at[pl.ds(me, 1)], recv.at[pl.ds(me, 1)], own_sem)
    own.start()
    pl.semaphore_wait(barrier, devices - 1)

    def push(k, _):
        to = lax.rem(me + k, devices)
        pltpu.make_async_remote_copy(
            src_ref=send.at[pl.ds(to, 1)], dst_ref=recv.at[pl.ds(me, 1)], send_sem=send_sem, recv_sem=recv_sem,
            device_id=where_is(to, subs), device_id_type=MESH).start()
        return 0

    lax.fori_loop(1, devices, push, 0)
    own.wait()
    every = pltpu.make_async_remote_copy(
        src_ref=send.at[pl.ds(0, devices - 1)], dst_ref=recv.at[pl.ds(0, devices - 1)], send_sem=send_sem,
        recv_sem=recv_sem, device_id=where_is(me, subs), device_id_type=MESH)
    every.wait_recv()
    every.wait_send()


def call_exchange(send, devices, subs, number):
    return pl.pallas_call(
        functools.partial(exchange_kernel, devices, subs),
        out_shape=jax.ShapeDtypeStruct(send.shape, F32),
        in_specs=[VMEM_SPEC],
        out_specs=VMEM_SPEC,
        scratch_shapes=[pltpu.SemaphoreType.DMA] * 3,
        compiler_params=pltpu.CompilerParams(collective_id=number, has_side_effects=True),
        name="exchange",
    )(send)


PADZ = 32


def relayout_in(stage, dst, layers, rows, pitch, first, offset):
    blocks = stage.shape[2] // TILE

    def layer(l, _):
        base = (l + first) * (rows * pitch) + offset
        for xt in range(rows // 8):
            for zt in range(blocks):
                part = stage[l, xt * 8 : xt * 8 + 8, zt * TILE : (zt + 1) * TILE]
                dst[pl.ds(base + xt * 8 * pitch + zt, 8, stride=pitch), :] = part
        return 0

    lax.fori_loop(0, layers, layer, 0)


def solid_kernel(devices, subs, remote, temp, coef, surface, out, top_out,
                 stage, coef_stage, cur, nxt, coefs, sends, halos, load_sem, out_sem, send_sem, recv_sem):
    layers, rows, span = temp.shape
    blocks = span // TILE
    me = lax.axis_index(AXES[0]) * subs + lax.axis_index(AXES[1]) if remote else 5
    loads = [pltpu.make_async_copy(temp, stage, load_sem.at[0]), pltpu.make_async_copy(coef, coef_stage, load_sem.at[1])]
    for load in loads:
        load.start()
    if remote:
        barrier = pltpu.get_barrier_semaphore()

        for by in (1, devices - 1):
            pl.semaphore_signal(barrier, inc=1, device_id=where_is(lax.rem(me + by, devices), subs), device_id_type=MESH)

    def clear(l, _):
        for x in range(rows):
            base = pl.multiple_of((l * rows + x) * PADZ, 8)
            for buf in (cur, nxt):
                buf[pl.ds(base, 8), :] = jnp.zeros((8, TILE), F32)
                buf[pl.ds(base + 24, 8), :] = jnp.zeros((8, TILE), F32)
        return 0

    lax.fori_loop(0, layers + 2, clear, 0)
    for l in (0, layers + 1):
        for buf in (cur, nxt):
            buf[l * rows * PADZ : (l + 1) * rows * PADZ, :] = jnp.zeros((rows * PADZ, TILE), F32)

    for side, edge in ((0, 0), (1, devices - 1)):
        @pl.when(me == edge)
        def _():
            halos[:, side] = jnp.zeros((SUBSTEPS,) + halos.shape[2:], F32)

    def copies(k):
        return [pltpu.make_async_remote_copy(
            src_ref=sends.at[k, side], dst_ref=halos.at[k, 1 - side], send_sem=send_sem.at[k, side],
            recv_sem=recv_sem.at[k, 1 - side], device_id=where_is(me - 1 if side == 0 else me + 1, subs),
            device_id_type=MESH) for side in (0, 1)]

    has = (me > 0, me < devices - 1)

    def launch(k):
        if remote:
            for side in (0, 1):
                @pl.when(has[side])
                def _():
                    copies(k)[side].start()

    def arrive(k):
        if remote:
            for side in (0, 1):
                @pl.when(has[side])
                def _():
                    copies(k)[1 - side].wait_recv()

    def drain(k):
        if remote:
            for side in (0, 1):
                @pl.when(has[side])
                def _():
                    copies(k)[side].wait_send()

    loads[0].wait()
    relayout_in(stage, cur, layers, rows, PADZ, 1, 8)

    def edges(l, _):
        for side, x in ((0, 0), (1, rows - 1)):
            base = pl.multiple_of(((l + 1) * rows + x) * PADZ + 8, 8)
            sends[0, side, l] = cur[pl.ds(base, blocks), :]
        return 0

    lax.fori_loop(0, layers, edges, 0)
    if remote:
        pl.semaphore_wait(barrier, 2)
    launch(0)
    loads[1].wait()
    relayout_in(coef_stage, coefs, layers, rows, blocks, 0, 0)

    lane = lax.broadcasted_iota(I32, (blocks, TILE), 1)
    first_lane, last_lane = lane == 0, lane == TILE - 1

    def advance(k, src, dst, chosen):
        def layer(l, _):
            zero = jnp.where(l == 0, 1.0 / SUBSTEPS, 0.0)

            def at(step, x, shift=0):
                start = (l + 1 + step) * (rows * PADZ) + (x * PADZ + 8 + shift)
                return src[pl.ds(start, blocks), :]

            for x in chosen:
                center = at(0, x)
                after = pltpu.roll(jnp.where(first_lane, at(0, x, 1), center), TILE - 1, 1)
                before = pltpu.roll(jnp.where(last_lane, at(0, x, -1), center), 1, 1)
                above = halos[k, 0, l] if x == 0 else at(0, x - 1)
                below = halos[k, 1, l] if x == rows - 1 else at(0, x + 1)
                beside = (at(-1, x) + at(1, x)) + (above + below) + (after + before)
                c = coefs[pl.ds(pl.multiple_of(l * (rows * blocks) + x * blocks, 8), blocks), :]
                value = center + c * (beside - 6.0 * center)
                value = value + zero * surface[x * blocks : (x + 1) * blocks, :]
                base = (l + 1) * (rows * PADZ) + (x * PADZ + 8)
                dst[pl.ds(pl.multiple_of(base, 8), blocks), :] = value
                if k + 1 < SUBSTEPS and x in (0, rows - 1):
                    sends[k + 1, 0 if x == 0 else 1, l] = value
            return 0

        lax.fori_loop(0, layers, layer, 0)

    for k in range(SUBSTEPS):
        src, dst = (cur, nxt) if k % 2 == 0 else (nxt, cur)
        arrive(k)
        advance(k, src, dst, (0, rows - 1))
        if k + 1 < SUBSTEPS:
            launch(k + 1)
        advance(k, src, dst, tuple(range(1, rows - 1)))

    final = cur if SUBSTEPS % 2 == 0 else nxt

    def back(l, _):
        base = (l + 1) * (rows * PADZ) + 8
        for xt in range(rows // 8):
            for zt in range(blocks):
                stage[l, xt * 8 : xt * 8 + 8, zt * TILE : (zt + 1) * TILE] = final[pl.ds(base + xt * 8 * PADZ + zt, 8, stride=PADZ), :]
        return 0

    lax.fori_loop(0, layers, back, 0)
    store = pltpu.make_async_copy(stage, out, out_sem)
    store.start()
    for x in range(rows):
        base = rows * PADZ + x * PADZ + 8
        top_out[x * blocks : (x + 1) * blocks, :] = final[base : base + blocks, :]
    for k in range(SUBSTEPS):
        drain(k)
    store.wait()


def call_solid(temp, coef, surface, devices, subs, number, remote=True):
    layers, rows, span = temp.shape
    blocks = span // TILE
    return pl.pallas_call(
        functools.partial(solid_kernel, devices, subs, remote),
        out_shape=(jax.ShapeDtypeStruct(temp.shape, F32), jax.ShapeDtypeStruct(surface.shape, F32)),
        in_specs=[ANY_SPEC, ANY_SPEC, VMEM_SPEC],
        out_specs=(ANY_SPEC, VMEM_SPEC),
        scratch_shapes=[
            pltpu.VMEM(temp.shape, F32),
            pltpu.VMEM(temp.shape, F32),
            pltpu.VMEM(((layers + 2) * rows * PADZ, TILE), F32),
            pltpu.VMEM(((layers + 2) * rows * PADZ, TILE), F32),
            pltpu.VMEM((layers * rows * blocks, TILE), F32),
            pltpu.VMEM((SUBSTEPS, 2, layers, blocks, TILE), F32),
            pltpu.VMEM((SUBSTEPS, 2, layers, blocks, TILE), F32),
            pltpu.SemaphoreType.DMA((2,)),
            pltpu.SemaphoreType.DMA,
            pltpu.SemaphoreType.DMA((SUBSTEPS, 2)),
            pltpu.SemaphoreType.DMA((SUBSTEPS, 2)),
        ],
        compiler_params=pltpu.CompilerParams(
            **(dict(collective_id=number) if remote else {}), has_side_effects=True, vmem_limit_bytes=60 << 20),
        name="solid",
    )(temp, coef, surface)


def from_behind(value, axis, by):
    length = lax.axis_size(axis)
    return lax.ppermute(value, axis, [(i, (i + by) % length) for i in range(length)])


def on_device(positions, particle_temp, pair_list, pair_count, ghost_particle, ghost_owner, ghost_cell,
              wall_seen, solid_temp, conduct):
    devices = lax.axis_size(AXES[0]) * lax.axis_size(AXES[1])
    subs = lax.axis_size(AXES[1])
    own_temp = particle_temp.reshape(-1, TILE)
    near_pos, near_temp = from_behind((positions, own_temp), AXES[1], -1)
    codes = pair_list[:, 0] * 32 + pair_list[:, 1]
    owner = ghost_owner.reshape(-1, TILE)
    heated, send, rank = call_particles(
        codes, pair_count, positions, own_temp, near_pos, near_temp, ghost_particle.reshape(-1, TILE),
        owner, ghost_cell.reshape(-1, TILE), wall_seen.reshape(-1, TILE), devices)
    recv = call_exchange(send, devices, subs, 0)
    surface = call_spread(recv, solid_temp.shape[1] * solid_temp.shape[2])
    temp, top = call_solid(solid_temp, conduct, surface, devices, subs, 1)
    values = call_pick(top, recv)
    back = call_exchange(values, devices, subs, 2)
    ghost = call_unpack(back, owner, rank)
    return heated.reshape(-1), temp, ghost.reshape(-1)


def solution(mesh):
    one, rows, plate = P(AXES), P(AXES, None), P(None, AXES, None)
    return jax.shard_map(
        on_device,
        mesh=mesh,
        in_specs=(P(None, AXES), one, rows, one, one, rows, one, one, plate, plate),
        out_specs=(one, plate, one),
        check_vma=False,
    )
```

time: 468 us -> 137 us (0.29); the launches traced: 459 us -> 138 us
  other arithmetic: 189 us -> 1.33 us
  local copies, waits for them, and re-layouts: 154 us -> 5.3 us
  Pallas kernels: 0 us -> 126 us
  starting transfers between devices: 76.7 us -> 3.7 us
  waiting for transfers between devices: 37.1 us -> 0.01 us
    pallas_call x0 -> x7, Pallas kernels: none -> 126 us  [the longest x1 61.1 us: call_solid(): pl.pallas_call(functools.partial(solid_kernel, devices, subs, remote), ou...]
    gather x67 -> x0, local copies, waits for them, and re-layouts: 92.1 us -> none  [the longest x1 23 us: on_device(): surface_now = temp[0].reshape(-1)[cell_index]]
    add x12 -> x1, other arithmetic: 70.1 us -> 1.33 us  [on_device(): codes = pair_list[:, 0] * 32 + pair_list[:, 1]]
    concatenate x8 -> x0, other arithmetic: 44.6 us -> none  [the longest x6 44.6 us: extended(): jnp.concatenate([jnp.pad(low, around), value, jnp.pad(high, around)], axi...]
    all_to_all x3 -> x0, starting transfers between devices: 42.8 us -> none  [exchange_both(): lax.all_to_all(pieces, axis, split_axis=0, concat_axis=0, tiled=True)]
    scatter-add x17 -> x0, other arithmetic: 36 us -> none  [the longest x1 24.7 us: on_device(): surface = jnp.zeros((slab_width * span_z,), jnp.float32).at[cell_index].a...]
    ppermute x12 -> x0, starting transfers between devices: 30.2 us -> none  [the longest x6 16 us: extended(): lax.ppermute(leading, axis, [(b, a) for a, b in up])]
    ppermute x12 -> x0, waiting for transfers between devices: 27.5 us -> none  [the longest x6 25.3 us: extended(): lax.ppermute(leading, axis, [(b, a) for a, b in up])]
  transfers between devices with their start and end apart: 17 -> 2, of which waited for: 11 -> 0; matrix products, arithmetic and copies ran while one was open for 34% -> 1% of each run, Pallas kernels for 0% -> 0%
where the time goes in v1:
time: 137 us; the launch traced here: 138 us
  Pallas kernels  126 us (92%)
  local copies, waits for them, and re-layouts  5.3 us (4%)
  starting transfers between devices  3.7 us (3%)
    pallas_call x1, Pallas kernels, call_solid(): pl.pallas_call(functools.partial(solid_kernel, devices, subs, remote), ou...  61.1 us
    pallas_call x2, Pallas kernels, call_exchange(): pl.pallas_call(functools.partial(exchange_kernel, devices, subs), out_sha...  45.3 us
    pallas_call x1, Pallas kernels, call_particles(): pl.pallas_call(particles_kernel, out_shape=(jax.ShapeDtypeStruct(own_temp...  9.91 us
    unnamed x5, local copies, waits for them, and re-layouts  5.3 us
    pallas_call x1, Pallas kernels, call_spread(): pl.pallas_call(spread_kernel, out_shape=jax.ShapeDtypeStruct((rows, TILE)...  4.26 us
    ppermute x2, starting transfers between devices, from_behind(): lax.ppermute(value, axis, [(i, (i + by) % length) for i in range(length)])  3.7 us
    pallas_call x1, Pallas kernels, call_pick(): pl.pallas_call(pick_kernel, out_shape=jax.ShapeDtypeStruct(recv.shape, F3...  3.54 us
  transfers between devices with their start and end apart: 2, of which 0 were waited for; matrix products, arithmetic and copies ran while one was open for 1% of the time, Pallas kernels for 0%

profile of v1, /device:TPU:1, one launch (start us, length us, event | category | flops | bytes accessed | tf_op | source)
XLA Modules:
  0.0 137.6 jit_solution(43827838993357534)
XLA Ops:
  0.6 1.4 %collective-permute-start.1 = (f32[16,128]{1,0:T(8,128)}, f32[16,128]{1,0:T(8,128)S(1)}, u32[]{:S(2)}, u32[]{:S(2)}) collective-permute-start(f32[16,128]{1,0:T(8,128)} %bitcast.10), channel_id=1, source_target_pairs={{0,7},{1,0},{2,1},{3,2},{4,3},{5,4},{6,5},{7,6},{8,15},{9,8},{10,9... | collective-permute-start | bytes 24584 | tf_op jit(solution)/shard_map/ppermute | solution.py:484
  2.0 2.3 %collective-permute-start = (f32[3,2048]{1,0:T(4,128)}, f32[3,2048]{1,0:T(4,128)S(1)}, u32[]{:S(2)}, u32[]{:S(2)}) collective-permute-start(f32[3,2048]{1,0:T(4,128)} %own_pos.1), channel_id=1, source_target_pairs={{0,7},{1,0},{2,1},{3,2},{4,3},{5,4},{6,5},{7,6},{8,15},{9,8},{10,9... | collective-permute-start | bytes 73736 | tf_op jit(solution)/shard_map/ppermute | solution.py:484
  4.3 1.3 slice_add_fusion
  6.3 0.0 collective-permute-done.1.near_temp
  6.3 0.0 copy-start.1
  6.3 0.0 collective-permute-done.near_pos
  6.3 0.0 copy-start
  6.4 0.6 copy-done.1
  6.9 0.0 copy-done
  7.0 9.9 %particles.1 = (f32[16,128]{1,0:T(8,128)}, f32[128,128]{1,0:T(8,128)}, s32[16,128]{1,0:T(8,128)}) custom-call(s32[256]{0:T(256)} %bitcast.16, s32[1]{0:T(128)S(6)} %copy.14.count, f32[3,2048]{1,0:T(4,128)} %own_pos.1, f32[16,128]{1,0:T(8,128)} %bitcast.11, f32[3,2048]{1,0:T(4,128)} %copy-done, f32[16,128]{1,0:T(8,128)} %copy-done.1, s32[16,128]{1,0:T(8,128)} %bitcast.12, ...), custom_call_target="tpu_custom_call" | custom-call | tf_op jit(solution)/shard_map/particles/pallas_call | solution.py:156
  16.9 19.0 %exchange.2.recv = f32[128,128]{1,0:T(8,128)} custom-call(f32[128,128]{1,0:T(8,128)} %get-tuple-element.9.send), custom_call_target="tpu_custom_call" | custom-call | tf_op jit(solution)/shard_map/exchange/pallas_call | solution.py:293
  35.9 4.3 %spread.1.surface = f32[256,128]{1,0:T(8,128)} custom-call(f32[128,128]{1,0:T(8,128)} %exchange.2.recv), custom_call_target="tpu_custom_call" | custom-call | tf_op jit(solution)/shard_map/spread/pallas_call | solution.py:195
  40.2 61.1 %solid.1 = (f32[32,16,2048]{2,1,0:T(8,128)}, f32[256,128]{1,0:T(8,128)}) custom-call(f32[32,16,2048]{2,1,0:T(8,128)} %temp.1, f32[32,16,2048]{2,1,0:T(8,128)} %coef.1, f32[256,128]{1,0:T(8,128)} %spread.1.surface), custom_call_target="tpu_custom_call" | custom-call | tf_op jit(solution)/shard_map/solid/pallas_call | solution.py:458
  101.3 3.5 %pick.1.send = f32[128,128]{1,0:T(8,128)} custom-call(f32[256,128]{1,0:T(8,128)} %get-tuple-element.11.surface, f32[128,128]{1,0:T(8,128)} %exchange.2.recv), custom_call_target="tpu_custom_call" | custom-call | tf_op jit(solution)/shard_map/pick/pallas_call | solution.py:223
  104.9 26.2 %exchange.3.values = f32[128,128]{1,0:T(8,128)} custom-call(f32[128,128]{1,0:T(8,128)} %pick.1.send), custom_call_target="tpu_custom_call" | custom-call | tf_op jit(solution)/shard_map/exchange/pallas_call | solution.py:293
  131.1 1.8 %unpack.1 = f32[16,128]{1,0:T(8,128)} custom-call(f32[128,128]{1,0:T(8,128)} %exchange.3.values, s32[16,128]{1,0:T(8,128)} %bitcast.9, s32[16,128]{1,0:T(8,128)} %get-tuple-element.12.rank), custom_call_target="tpu_custom_call" | custom-call | tf_op jit(solution)/shard_map/unpack/pallas_call | solution.py:246
  132.9 4.7 %copy.15 = f32[32,16,2048]{2,1,0:T(8,128)} copy(f32[32,16,2048]{2,1,0:T(8,128)} %get-tuple-element.17) | data formatting | bytes 8388608
Async XLA Ops:
  0.6 5.7 %collective-permute-start.1 = (f32[16,128]{1,0:T(8,128)}, f32[16,128]{1,0:T(8,128)S(1)}, u32[]{:S(2)}, u32[]{:S(2)}) collective-permute-start(f32[16,128]{1,0:T(8,128)} %bitcast.10), channel_id=1, source_target_pairs={{0,7},{1,0},{2,1},{3,2},{4,3},{5,4},{6,5},{7,6},{8,15},{9,8},{10,9... | collective-permute-start | bytes 24584 | tf_op jit(solution)/shard_map/ppermute | solution.py:484
  2.0 4.3 %collective-permute-start = (f32[3,2048]{1,0:T(4,128)}, f32[3,2048]{1,0:T(4,128)S(1)}, u32[]{:S(2)}, u32[]{:S(2)}) collective-permute-start(f32[3,2048]{1,0:T(4,128)} %own_pos.1), channel_id=1, source_target_pairs={{0,7},{1,0},{2,1},{3,2},{4,3},{5,4},{6,5},{7,6},{8,15},{9,8},{10,9... | collective-permute-start | bytes 73736 | tf_op jit(solution)/shard_map/ppermute | solution.py:484
  6.3 0.6 copy-start.1
  6.3 0.6 copy-start

commit v2 on v0

v2 whole, which is shorter than its diff:
```python
import functools
import jax
import jax.numpy as jnp
from jax import lax
from jax.experimental import pallas as pl
from jax.experimental.pallas import tpu as pltpu
from jax.sharding import PartitionSpec as P

F32, BF16, I32 = jnp.float32, jnp.bfloat16, jnp.int32
TILE = 128
SUBSTEPS = 6
SLOTS = 32
HEAT_RATE = 0.004
WALL_HEAT = 0.5
UNROLL = 8
CHUNKS = 4
AXES = ("fluid", "sub")
VMEM_SPEC = pl.BlockSpec(memory_space=pltpu.VMEM)
SMEM_SPEC = pl.BlockSpec(memory_space=pltpu.SMEM)
ANY_SPEC = pl.BlockSpec(memory_space=pl.ANY)


def split3(x):
    high = x.astype(BF16).astype(F32)
    rest = x - high
    mid = rest.astype(BF16).astype(F32)
    return high, mid, rest - mid


def row_of(ref):
    return jnp.concatenate([ref[t : t + 1, :] for t in range(ref.shape[0])], axis=1)


def onehot(rows, codes, dtype=BF16):
    shape = (rows, codes.shape[1])
    hit = lax.broadcasted_iota(I32, shape, 0) == jnp.broadcast_to(codes, shape)
    return jnp.where(hit, 1.0, 0.0).astype(dtype)


def dot_nn(a, b):
    return lax.dot_general(a, b, (((1,), (0,)), ((), ())), preferred_element_type=F32)


def dot_nt(a, b):
    return lax.dot_general(a, b, (((1,), (1,)), ((), ())), preferred_element_type=F32)


def put_features(pos, temp_row, left, right):
    wide = pos.shape[1]
    moved = pos - 0.5
    high, mid, low = split3(moved)
    squares = jnp.sum(moved * moved, axis=0, keepdims=True)
    one = jnp.ones((3, wide), F32)
    minus = split3(-squares)
    temps = split3(temp_row)
    for place, part in enumerate((high, high, mid, mid, high, low)):
        left[3 * place : 3 * place + 3, :] = part
    left[18:21, :] = one
    for k in range(3):
        left[21 + k : 22 + k, :] = minus[k]
        left[24 + k : 25 + k, :] = temps[k]
    left[27:30, :] = one
    left[30:32, :] = jnp.zeros((2, wide), F32)
    if right is None:
        return
    base = split3(1.0 - squares)
    for place, part in enumerate((high, mid, high, mid, low, high)):
        right[3 * place : 3 * place + 3, :] = 2.0 * part
    right[21:24, :] = one
    right[24:27, :] = one
    for k in range(3):
        right[18 + k : 19 + k, :] = base[k]
        right[27 + k : 28 + k, :] = -temps[k]
    right[30:32, :] = jnp.zeros((2, wide), F32)


def ranks(owners, devices):
    row = lax.broadcasted_iota(I32, (TILE, 2 * TILE), 0)
    col = lax.broadcasted_iota(I32, (TILE, 2 * TILE), 1)
    before = jnp.where((row < col) | (col >= TILE), 1.0, 0.0).astype(BF16)
    so_far = jnp.zeros((devices, TILE), F32)
    out = []
    for t in range(owners.shape[1] // TILE):
        mine = owners[:, t * TILE : (t + 1) * TILE]
        counted = dot_nn(mine, before)
        out.append(jnp.sum(mine.astype(F32) * (counted[:, :TILE] + so_far), axis=0, keepdims=True))
        so_far = so_far + counted[:, TILE:]
    return jnp.concatenate(out, axis=1)


def plate_row(code):
    return (lax.shift_right_logical(code, 7) & 15) * 16 + lax.shift_right_logical(code, 11)


LOW, TOP = 7, 8


def stencil_weights():
    row = lax.broadcasted_iota(I32, (2 * TILE, 2 * TILE), 0) & (TILE - 1)
    col = lax.broadcasted_iota(I32, (2 * TILE, 2 * TILE), 1)
    lane = col & (TILE - 1)
    near = jnp.where(jnp.abs(row - lane) == 1, 1.0, jnp.where(row == lane, -6.0, 0.0))
    swap = jnp.where((jnp.abs(row - lane) == TILE - 1), 1.0, 0.0)
    return jnp.where(col < TILE, near, swap).astype(BF16)


MESH = pl.DeviceIdType.MESH


def step_kernel(
    fluids, subs, codes, own_pos, own_temp, code_rows, count, which, owner, cell, seen, temp, coef,
    heated, out, ghost_out,
    left, right, lefts, rights, partial, near_pos, near_temp, owners, rank_row, send, recv, hot, lows, source,
    values, back, cur, nxt, coefs, weights,
    near_send, near_recv, first_send, first_recv, last_send, last_recv, own_sem, load_sem, out_sem, send_sem, recv_sem,
):
    devices = fluids * subs
    layers, rows, span = temp.shape
    blocks = span // TILE
    tiles = own_temp.shape[0]
    deep = layers // CHUNKS
    fluid, sub = lax.axis_index(AXES[0]), lax.axis_index(AXES[1])
    me = fluid * subs + sub

    def place(index):
        return (lax.div(index, subs), lax.rem(index, subs))

    def everyone(act):
        for by in range(1, subs):
            act(fluid, lax.rem(sub + by, subs))

        def row(up, _):
            other = lax.rem(fluid + up, fluids)
            for by in range(subs):
                act(other, lax.rem(sub + by, subs))
            return 0

        lax.fori_loop(1, fluids, row, 0)

    loads = []
    for array, buf, offset in ((temp, cur, 1), (coef, coefs, 0)):
        for zt in range(blocks):
            at = pl.ds(zt * TILE, TILE)
            where = pl.ds(TOP, rows) if offset else pl.ds(0, rows)
            loads.append(pltpu.make_async_copy(
                array.at[:, :, at], buf.at[pl.ds(offset, layers), zt, where, :], load_sem.at[1 - offset, zt]))
    for load in loads:
        load.start()

    barrier = pltpu.get_barrier_semaphore()
    everyone(lambda f, s: pl.semaphore_signal(barrier, inc=1, device_id=(f, s), device_id_type=MESH))

    weights[...] = stencil_weights()
    for l in (0, layers + 1):
        for buf in (cur, nxt):
            for zt in range(blocks):
                buf[l, zt, TOP : TOP + rows, :] = jnp.zeros((rows, TILE), F32)

    for edge, x in ((0, LOW), (devices - 1, TOP + rows)):
        @pl.when(me == edge)
        def _():
            def wipe(l, _):
                for buf in (cur, nxt):
                    for zt in range(blocks):
                        buf[l, zt, x : x + 1, :] = jnp.zeros((1, TILE), F32)
                return 0

            lax.fori_loop(1, layers + 1, wipe, 0)

    put_features(own_pos[...], row_of(own_temp), left, right)
    for t in range(tiles):
        lefts[t] = left[:, t * TILE : (t + 1) * TILE].T.astype(BF16)
        block = right[:, t * TILE : (t + 1) * TILE]
        upper = lax.broadcasted_iota(I32, block.shape, 0) < 24
        rights[t, :, 0:TILE] = jnp.where(upper, block, 0.0).astype(BF16)
        rights[t, :, TILE : 2 * TILE] = jnp.where(upper, 0.0, block).astype(BF16)

    def halo(k, side, c):
        buf = (cur, nxt)[k % 2]
        x, y = ((TOP, TOP + rows), (TOP + rows - 1, LOW))[side]
        at = pl.ds(1 + c * deep, deep)
        return pltpu.make_async_remote_copy(
            src_ref=buf.at[at, :, pl.ds(x, 1), :], dst_ref=buf.at[at, :, pl.ds(y, 1), :],
            send_sem=send_sem.at[k, side, c], recv_sem=recv_sem.at[k, 1 - side, c],
            device_id=place(me - 1 if side == 0 else me + 1), device_id_type=MESH)

    has = (me > 0, me < devices - 1)

    def each(act):
        for side in (0, 1):
            @pl.when(has[side])
            def _():
                act(side)

    def launch(k, c):
        each(lambda side: halo(k, side, c).start())

    def arrive(k, c):
        each(lambda side: halo(k, 1 - side, c).wait_recv())

    def drain(k, c):
        each(lambda side: halo(k, side, c).wait_send())

    pl.semaphore_wait(barrier, devices - 1)
    behind = (fluid, lax.rem(sub + subs - 1, subs))
    near = [pltpu.make_async_remote_copy(
        src_ref=src, dst_ref=dst, send_sem=near_send.at[n], recv_sem=near_recv.at[n], device_id=behind,
        device_id_type=MESH) for n, (src, dst) in enumerate(((own_pos, near_pos), (own_temp, near_temp)))]
    for copy in near:
        copy.start()
    for load in loads[:blocks]:
        load.wait()
    for c in range(CHUNKS):
        launch(0, c)

    owners[...] = onehot(devices, row_of(owner))
    rank_row[...] = ranks(owners[...], devices)

    for copy in near:
        copy.wait_recv()
    put_features(near_pos[...], row_of(near_temp), left, None)
    for t in range(tiles):
        lefts[tiles + t] = left[:, t * TILE : (t + 1) * TILE].T.astype(BF16)

    def pair_group(group, _):
        for k in range(UNROLL):
            number = group * UNROLL + k
            code = codes[number]
            first = lax.shift_right_logical(code, 5) & (tiles - 1)
            second = code & (2 * tiles - 1)
            both = dot_nn(lefts[second], rights[first])
            close = jnp.maximum(both[:, :TILE], 0.0)
            gained = close * close * both[:, TILE:]
            partial[pl.ds(pl.multiple_of(number * 8, 8), 8), :] = jnp.sum(gained.reshape(TILE // 8, 8, TILE), axis=0)
        return 0

    pairs = codes.shape[0]
    lax.fori_loop(0, pairs // UNROLL, pair_group, 0)
    summed = partial[pl.ds(0, pairs, stride=8), :]
    for s in range(1, 8):
        summed = summed + partial[pl.ds(s, pairs, stride=8), :]
    code_row = row_of(code_rows)
    number = lax.broadcasted_iota(I32, code_row.shape, 1)
    first = jnp.where(number < count[0], lax.shift_right_logical(code_row, 5) & (tiles - 1), -1)
    firsts = onehot(tiles, first)
    gain = jnp.zeros((tiles, TILE), F32)
    for part in split3(summed):
        gain = gain + dot_nn(firsts, part.astype(BF16))
    out_temp = own_temp[...] + HEAT_RATE * gain
    heated[...] = out_temp

    parts = jnp.concatenate(split3(out_temp), axis=0).T.astype(BF16)
    which_row = row_of(which)
    high = onehot(tiles, lax.shift_right_logical(which_row, 7))
    picked = dot_nn(parts, jnp.concatenate([high] * 3, axis=0))
    low = jnp.broadcast_to(which_row & (TILE - 1), picked.shape)
    hit = lax.broadcasted_iota(I32, picked.shape, 0) == low
    flux = WALL_HEAT * (jnp.sum(jnp.where(hit, picked, 0.0), axis=0, keepdims=True) - row_of(seen))
    slot = onehot(SLOTS, rank_row[...].astype(I32), F32)
    cell_row = row_of(cell)
    cells = ((cell_row & ~255).astype(F32), (cell_row & 255).astype(F32), None)
    total = jnp.zeros((devices, 2 * SLOTS), F32)
    for f, c in zip(split3(flux), cells):
        lower_half = jnp.zeros_like(slot) if c is None else slot * c
        total = total + dot_nt(owners[...], jnp.concatenate([slot * f, lower_half], axis=0).astype(BF16))
    send[...] = jnp.concatenate([total, jnp.zeros((devices, TILE - 2 * SLOTS), F32)], axis=1)

    def spread_out(src, dst, sends, recvs):
        everyone(lambda f, s: pltpu.make_async_remote_copy(
            src_ref=src.at[pl.ds(f * subs + s, 1)], dst_ref=dst.at[pl.ds(me, 1)], send_sem=sends, recv_sem=recvs,
            device_id=(f, s), device_id_type=MESH).start())
        return pltpu.make_async_remote_copy(
            src_ref=src.at[pl.ds(0, devices - 1)], dst_ref=dst.at[pl.ds(0, devices - 1)], send_sem=sends,
            recv_sem=recvs, device_id=behind, device_id_type=MESH)

    own = pltpu.make_async_copy(send.at[pl.ds(me, 1)], recv.at[pl.ds(me, 1)], own_sem.at[0])
    own.start()
    first_trip = spread_out(send, recv, first_send, first_recv)

    for load in loads[blocks:]:
        load.wait()
    lane = lax.broadcasted_iota(I32, (rows, TILE), 1)
    lower = lane < TILE // 2

    def advance(src, dst, c):
        def layer(n, _):
            l = c * deep + n
            high, low = [], []
            for zt in range(blocks):
                center = src[l + 1, zt, TOP : TOP + rows, :]
                part = center.astype(BF16)
                high.append(part)
                low.append((center - part.astype(F32)).astype(BF16))
            both = jnp.concatenate([jnp.concatenate(high, axis=0), jnp.concatenate(low, axis=0)], axis=1)
            both = dot_nn(both, weights[...])
            along = [both[zt * rows : (zt + 1) * rows, :TILE] for zt in range(blocks)]
            ends = [both[zt * rows : (zt + 1) * rows, TILE:] for zt in range(blocks)]
            nothing = jnp.zeros((rows, TILE), F32)
            for zt in range(blocks):
                end = jnp.where(lower, ends[zt - 1] if zt > 0 else nothing, ends[zt + 1] if zt + 1 < blocks else nothing)
                beside = src[l, zt, TOP : TOP + rows, :] + src[l + 2, zt, TOP : TOP + rows, :]
                beside = beside + (src[l + 1, zt, LOW : LOW + rows, :] + src[l + 1, zt, TOP + 1 : TOP + 1 + rows, :])
                beside = beside + (along[zt] + end)
                dst[l + 1, zt, TOP : TOP + rows, :] = src[l + 1, zt, TOP : TOP + rows, :] + coefs[l, zt] * beside
            return 0

        lax.fori_loop(0, deep, layer, 0, unroll=4)

    def heat_top(dst):
        for zt in range(blocks):
            dst[1, zt, TOP : TOP + rows, :] += source[zt * rows : (zt + 1) * rows, :]

    def step(k):
        src, dst = (cur, nxt) if k % 2 == 0 else (nxt, cur)

        def chunk(c, _):
            arrive(k, c)
            if k > 0:
                drain(k - 1, c)
            advance(src, dst, c)
            if k == 0:
                @pl.when(c > 0)
                def _():
                    launch(1, c)
            elif k + 1 < SUBSTEPS:
                @pl.when(c == 0)
                def _():
                    heat_top(dst)

                launch(k + 1, c)
            else:
                @pl.when(c == 0)
                def _():
                    heat_top(dst)
            return 0

        lax.fori_loop(0, CHUNKS, chunk, 0)

    def stores(c):
        at = pl.ds(c * deep, deep)
        return [pltpu.make_async_copy(
            cur.at[pl.ds(1 + c * deep, deep), zt, pl.ds(TOP, rows), :], out.at[at, :, pl.ds(zt * TILE, TILE)],
            out_sem.at[c, zt]) for zt in range(blocks)]

    step(0)

    own.wait()
    first_trip.wait_recv()
    turned = recv[...].T
    for s in range(SLOTS):
        code = turned[SLOTS + s : SLOTS + s + 1, :].astype(I32)
        flux = turned[s : s + 1, :] * (1.0 / SUBSTEPS)
        at = pl.ds(s * devices, devices)
        hot[:, at] = onehot(hot.shape[0], plate_row(code))
        low = onehot(TILE, code & (TILE - 1), F32)
        for k, part in enumerate(split3(flux)):
            lows[k, :, at] = (low * part).astype(BF16)
    total = dot_nt(hot[...], lows[0])
    total = total + dot_nt(hot[...], lows[1])
    source[...] = total + dot_nt(hot[...], lows[2])
    heat_top(nxt)
    launch(1, 0)

    for k in range(1, SUBSTEPS - 1):
        step(k)

    last = SUBSTEPS - 1
    arrive(last, 0)
    drain(last - 1, 0)
    advance(nxt, cur, 0)
    heat_top(cur)
    for store in stores(0):
        store.start()
    flat = jnp.concatenate([cur[1, zt, TOP : TOP + rows, :] for zt in range(blocks)], axis=0)
    wide = jnp.concatenate([flat[k : k + TILE, :].T for k in range(0, flat.shape[0], TILE)], axis=1)
    parts = [part.astype(BF16) for part in split3(wide)]
    found_rows = []
    for s in range(SLOTS):
        at = pl.ds(s * devices, devices)
        found = sum(dot_nn(part, hot[:, at]) for part in parts)
        code = turned[SLOTS + s : SLOTS + s + 1, :].astype(I32)
        low = lax.broadcasted_iota(I32, found.shape, 0) == jnp.broadcast_to(code & (TILE - 1), found.shape)
        found_rows.append(jnp.sum(jnp.where(low, found, 0.0), axis=0, keepdims=True))
    found_rows.append(jnp.zeros((TILE - SLOTS, devices), F32))
    values[...] = jnp.concatenate(found_rows, axis=0).T
    own = pltpu.make_async_copy(values.at[pl.ds(me, 1)], back.at[pl.ds(me, 1)], own_sem.at[1])
    own.start()
    last_trip = spread_out(values, back, last_send, last_recv)

    def closing(c, _):
        arrive(last, c)
        drain(last - 1, c)
        advance(nxt, cur, c)
        for store in stores(c):
            store.start()
        return 0

    lax.fori_loop(1, CHUNKS, closing, 0)

    own.wait()
    last_trip.wait_recv()
    found = dot_nn(jnp.concatenate(split3(back[...].T[0:SLOTS, :]), axis=0).astype(BF16), owners[...])
    found = found[0:SLOTS] + found[SLOTS : 2 * SLOTS] + found[2 * SLOTS :]
    slot = onehot(SLOTS, rank_row[...].astype(I32), F32)
    ghost = jnp.sum(found * slot, axis=0, keepdims=True)
    for t in range(ghost_out.shape[0]):
        ghost_out[t : t + 1, :] = ghost[:, t * TILE : (t + 1) * TILE]

    for copy in near:
        copy.wait_send()
    first_trip.wait_send()
    last_trip.wait_send()
    for c in range(CHUNKS):
        drain(last, c)
    for c in range(CHUNKS):
        for store in stores(c):
            store.wait()


def call_step(codes, count, own_pos, own_temp, which, owner, cell, seen, temp, coef, fluids, subs):
    devices = fluids * subs
    layers, rows, span = temp.shape
    blocks = span // TILE
    tiles, wide = own_temp.shape[0], own_pos.shape[1]
    ghosts = owner.shape[0] * TILE
    DMA = pltpu.SemaphoreType.DMA
    return pl.pallas_call(
        functools.partial(step_kernel, fluids, subs),
        out_shape=(
            jax.ShapeDtypeStruct(own_temp.shape, F32),
            jax.ShapeDtypeStruct(temp.shape, F32),
            jax.ShapeDtypeStruct(owner.shape, F32),
        ),
        in_specs=[SMEM_SPEC] + [VMEM_SPEC] * 3 + [SMEM_SPEC] + [VMEM_SPEC] * 4 + [ANY_SPEC] * 2,
        out_specs=(VMEM_SPEC, ANY_SPEC, VMEM_SPEC),
        scratch_shapes=[
            pltpu.VMEM((32, wide), F32),
            pltpu.VMEM((32, wide), F32),
            pltpu.VMEM((2 * tiles, TILE, 32), BF16),
            pltpu.VMEM((tiles, 32, 2 * TILE), BF16),
            pltpu.VMEM((codes.shape[0] * 8, TILE), F32),
            pltpu.VMEM(own_pos.shape, F32),
            pltpu.VMEM(own_temp.shape, F32),
            pltpu.VMEM((devices, ghosts), BF16),
            pltpu.VMEM((1, ghosts), F32),
            pltpu.VMEM((devices, TILE), F32),
            pltpu.VMEM((devices, TILE), F32),
            pltpu.VMEM((rows * blocks, devices * SLOTS), BF16),
            pltpu.VMEM((3, TILE, devices * SLOTS), BF16),
            pltpu.VMEM((rows * blocks, TILE), F32),
            pltpu.VMEM((devices, TILE), F32),
            pltpu.VMEM((devices, TILE), F32),
            pltpu.VMEM((layers + 2, blocks, TOP + rows + 8, TILE), F32),
            pltpu.VMEM((layers + 2, blocks, TOP + rows + 8, TILE), F32),
            pltpu.VMEM((layers, blocks, rows, TILE), F32),
            pltpu.VMEM((2 * TILE, 2 * TILE), BF16),
            DMA((2,)),
            DMA((2,)),
            DMA,
            DMA,
            DMA,
            DMA,
            DMA((2,)),
            DMA((2, blocks)),
            DMA((CHUNKS, blocks)),
            DMA((SUBSTEPS, 2, CHUNKS)),
            DMA((SUBSTEPS, 2, CHUNKS)),
        ],
        compiler_params=pltpu.CompilerParams(collective_id=0, has_side_effects=True, vmem_limit_bytes=60 << 20),
        name="step",
    )(codes, own_pos, own_temp, codes.reshape(-1, TILE), count, which, owner, cell, seen, temp, coef)


def on_device(positions, particle_temp, pair_list, pair_count, ghost_particle, ghost_owner, ghost_cell,
              wall_seen, solid_temp, conduct):
    codes = pair_list[:, 0] * 32 + pair_list[:, 1]

    def tiled(x):
        return x.reshape(-1, TILE)

    heated, temp, ghost = call_step(
        codes, pair_count, positions, tiled(particle_temp), tiled(ghost_particle), tiled(ghost_owner),
        tiled(ghost_cell), tiled(wall_seen), solid_temp, conduct, lax.axis_size(AXES[0]), lax.axis_size(AXES[1]))
    return heated.reshape(-1), temp, ghost.reshape(-1)


def solution(mesh):
    one, rows, plate = P(AXES), P(AXES, None), P(None, AXES, None)
    return jax.shard_map(
        on_device,
        mesh=mesh,
        in_specs=(P(None, AXES), one, rows, one, one, rows, one, one, plate, plate),
        out_specs=(one, plate, one),
        check_vma=False,
    )
```

time: 468 us -> 80.7 us (0.17); the launches traced: 459 us -> 80.4 us
  other arithmetic: 189 us -> 1.32 us
  local copies, waits for them, and re-layouts: 154 us -> 6.61 us
  starting transfers between devices: 76.7 us -> 0 us
  Pallas kernels: 0 us -> 71.2 us
  waiting for transfers between devices: 37.1 us -> 0 us
    gather x67 -> x0, local copies, waits for them, and re-layouts: 92.1 us -> none  [the longest x1 23 us: on_device(): surface_now = temp[0].reshape(-1)[cell_index]]
    pallas_call x0 -> x1, Pallas kernels: none -> 71.2 us  [call_step(): pl.pallas_call(functools.partial(step_kernel, fluids, subs), out_shape=(j...]
    add x12 -> x1, other arithmetic: 70.1 us -> 1.32 us  [on_device(): codes = pair_list[:, 0] * 32 + pair_list[:, 1]]
    concatenate x8 -> x0, other arithmetic: 44.6 us -> none  [the longest x6 44.6 us: extended(): jnp.concatenate([jnp.pad(low, around), value, jnp.pad(high, around)], axi...]
    all_to_all x3 -> x0, starting transfers between devices: 42.8 us -> none  [exchange_both(): lax.all_to_all(pieces, axis, split_axis=0, concat_axis=0, tiled=True)]
    scatter-add x17 -> x0, other arithmetic: 36 us -> none  [the longest x1 24.7 us: on_device(): surface = jnp.zeros((slab_width * span_z,), jnp.float32).at[cell_index].a...]
    ppermute x14 -> x0, starting transfers between devices: 33.9 us -> none  [the longest x6 16 us: extended(): lax.ppermute(leading, axis, [(b, a) for a, b in up])]
    ppermute x14 -> x0, waiting for transfers between devices: 27.5 us -> none  [the longest x6 25.3 us: extended(): lax.ppermute(leading, axis, [(b, a) for a, b in up])]
  transfers between devices with their start and end apart: 17 -> 0, of which waited for: 11 -> 0; matrix products, arithmetic and copies ran while one was open for 34% -> 0% of each run, Pallas kernels for 0% -> 0%
where the time goes in v2:
time: 80.7 us; the launch traced here: 80.4 us
  Pallas kernels  71.2 us (88%)
  local copies, waits for them, and re-layouts  6.61 us (8%)
  other arithmetic  1.32 us (2%)
  between operations  1.29 us (2%)
    pallas_call x1, Pallas kernels, call_step(): pl.pallas_call(functools.partial(step_kernel, fluids, subs), out_shape=(j...  71.2 us
    unnamed x5, local copies, waits for them, and re-layouts  6.61 us

profile of v2, /device:TPU:1, one launch (start us, length us, event | category | flops | bytes accessed | tf_op | source)
XLA Modules:
  0.0 80.4 jit_solution(12437335606353759745)
XLA Ops:
  1.3 1.3 %slice_add_fusion = s32[256,1]{0,1:T(1,128)} fusion(s32[256,2]{0,1:T(2,128)} %param.12), kind=kLoop, calls=%fused_computation | loop fusion | flops 512 | bytes 3072 | tf_op jit(solution)/shard_map/add | solution.py:476
  2.6 71.2 %step.1 = (f32[16,128]{1,0:T(8,128)}, f32[32,16,2048]{2,1,0:T(8,128)}, f32[16,128]{1,0:T(8,128)}) custom-call(s32[256]{0:T(256)} %bitcast.9, f32[3,2048]{1,0:T(4,128)} %own_pos.1, f32[16,128]{1,0:T(8,128)} %bitcast.13, s32[2,128]{1,0:T(2,128)} %bitcast.10, s32[1]{0:T(128)S(6)} %copy.16.count, s32[16,128]{1,0:T(8,128)} %bitcast.14, s32[16,128]{1,0:T(8,128)} %bitcast.15, ...), custom_call_target="tpu_custom_call" | custom-call | tf_op jit(solution)/shard_map/step/pallas_call | solution.py:427
  73.8 1.3 %copy.17 = f32[2048]{0:T(1024)} copy(f32[2048]{0:T(1024)} %bitcast.12) | data formatting | bytes 16384
  75.1 0.0 copy-start
  75.1 4.7 %copy.18 = f32[32,16,2048]{2,1,0:T(8,128)} copy(f32[32,16,2048]{2,1,0:T(8,128)} %get-tuple-element.13) | data formatting | bytes 8388608
  79.8 0.0 copy-done
  79.8 0.6 copy.19
Async XLA Ops:
  75.1 4.7 %copy-start = (f32[16,128]{1,0:T(8,128)S(1)}, f32[16,128]{1,0:T(8,128)}, u32[]{:S(2)}) copy-start(f32[16,128]{1,0:T(8,128)} %get-tuple-element.8) | copy-start | bytes 24580

commit v3 on v2

--- a/solution.py
+++ b/solution.py
@@ -12,12 +12,13 @@
 SLOTS = 32
 HEAT_RATE = 0.004
 WALL_HEAT = 0.5
-UNROLL = 8
+UNROLL = 16
 CHUNKS = 4
 AXES = ("fluid", "sub")
 VMEM_SPEC = pl.BlockSpec(memory_space=pltpu.VMEM)
 SMEM_SPEC = pl.BlockSpec(memory_space=pltpu.SMEM)
 ANY_SPEC = pl.BlockSpec(memory_space=pl.ANY)
+HBM_SPEC = pl.BlockSpec(memory_space=pltpu.HBM)
 
 
 def split3(x):
@@ -25,6 +26,11 @@
     rest = x - high
     mid = rest.astype(BF16).astype(F32)
     return high, mid, rest - mid
+
+
+def split2(x):
+    high = x.astype(BF16).astype(F32)
+    return high, x - high
 
 
 def row_of(ref):
@@ -59,19 +65,27 @@
     for k in range(3):
         left[21 + k : 22 + k, :] = minus[k]
         left[24 + k : 25 + k, :] = temps[k]
-    left[27:30, :] = one
-    left[30:32, :] = jnp.zeros((2, wide), F32)
+    left[27:32, :] = jnp.zeros((5, wide), F32)
     if right is None:
         return
     base = split3(1.0 - squares)
     for place, part in enumerate((high, mid, high, mid, low, high)):
         right[3 * place : 3 * place + 3, :] = 2.0 * part
-    right[21:24, :] = one
-    right[24:27, :] = one
     for k in range(3):
         right[18 + k : 19 + k, :] = base[k]
-        right[27 + k : 28 + k, :] = -temps[k]
-    right[30:32, :] = jnp.zeros((2, wide), F32)
+    right[21:24, :] = one
+    right[24:32, :] = jnp.zeros((8, wide), F32)
+
+
+def put_tile(left, t, tile, lefts, across):
+    block = left[:, t * TILE : (t + 1) * TILE]
+    block = jnp.concatenate([block] * 4, axis=0).T
+    lane = lax.broadcasted_iota(I32, block.shape, 1)
+    lefts[0, tile] = jnp.where(lane < 32, block, 0.0).astype(BF16)
+    lefts[1, tile] = jnp.where((lane >= 32) & (lane < 64), block, 0.0).astype(BF16)
+    row = lax.broadcasted_iota(I32, (TILE, TILE), 0)
+    take = jnp.where((row >= 24) & (row < 27), 1.0, 0.0).astype(BF16)
+    across[tile] = dot_nn(lefts[0, tile], take)
 
 
 def ranks(owners, devices):
@@ -108,11 +122,12 @@
 
 
 def step_kernel(
-    fluids, subs, codes, own_pos, own_temp, code_rows, count, which, owner, cell, seen, temp, coef,
+    fluids, subs, count, codes_in, pos_in, temp_in, which_in, owner_in, cell_in, seen_in, temp, coef,
     heated, out, ghost_out,
-    left, right, lefts, rights, partial, near_pos, near_temp, owners, rank_row, send, recv, hot, lows, source,
+    codes, code_rows, own_pos, own_temp, which, owner, cell, seen, small_sem,
+    left, right, lefts, across, rights, partial, near_pos, near_temp, owners, rank_row, send, recv, turned, found_rows, hot, lows, source,
     values, back, cur, nxt, coefs, weights,
-    near_send, near_recv, first_send, first_recv, last_send, last_recv, own_sem, load_sem, out_sem, send_sem, recv_sem,
+    near_send, near_recv, first_send, first_recv, last_send, last_recv, own_sem, load_sem, send_sem, recv_sem,
 ):
     devices = fluids * subs
     layers, rows, span = temp.shape
@@ -136,6 +151,12 @@
             return 0
 
         lax.fori_loop(1, fluids, row, 0)
+
+    small = [pltpu.make_async_copy(src, dst, small_sem.at[n]) for n, (src, dst) in enumerate((
+        (codes_in, codes), (codes_in, code_rows), (pos_in, own_pos), (temp_in, own_temp), (which_in, which),
+        (owner_in, owner), (cell_in, cell), (seen_in, seen)))]
+    for copy in small:
+        copy.start()
 
     loads = []
     for array, buf, offset in ((temp, cur, 1), (coef, coefs, 0)):
@@ -167,13 +188,12 @@
 
             lax.fori_loop(1, layers + 1, wipe, 0)
 
+    for copy in small:
+        copy.wait()
     put_features(own_pos[...], row_of(own_temp), left, right)
     for t in range(tiles):
-        lefts[t] = left[:, t * TILE : (t + 1) * TILE].T.astype(BF16)
-        block = right[:, t * TILE : (t + 1) * TILE]
-        upper = lax.broadcasted_iota(I32, block.shape, 0) < 24
-        rights[t, :, 0:TILE] = jnp.where(upper, block, 0.0).astype(BF16)
-        rights[t, :, TILE : 2 * TILE] = jnp.where(upper, 0.0, block).astype(BF16)
+        put_tile(left, t, t, lefts, across)
+        rights[t] = right[:, t * TILE : (t + 1) * TILE].astype(BF16)
 
     def halo(k, side, c):
         buf = (cur, nxt)[k % 2]
@@ -220,28 +240,34 @@
         copy.wait_recv()
     put_features(near_pos[...], row_of(near_temp), left, None)
     for t in range(tiles):
-        lefts[tiles + t] = left[:, t * TILE : (t + 1) * TILE].T.astype(BF16)
+        put_tile(left, t, tiles + t, lefts, across)
+
+    none = jnp.zeros((32, TILE), BF16)
 
     def pair_group(group, _):
-        for k in range(UNROLL):
+        for k in range(0, UNROLL, 2):
             number = group * UNROLL + k
-            code = codes[number]
-            first = lax.shift_right_logical(code, 5) & (tiles - 1)
-            second = code & (2 * tiles - 1)
-            both = dot_nn(lefts[second], rights[first])
-            close = jnp.maximum(both[:, :TILE], 0.0)
-            gained = close * close * both[:, TILE:]
-            partial[pl.ds(pl.multiple_of(number * 8, 8), 8), :] = jnp.sum(gained.reshape(TILE // 8, 8, TILE), axis=0)
+            first = [codes[0, number + n] & (tiles - 1) for n in (0, 1)]
+            second = [codes[1, number + n] & (2 * tiles - 1) for n in (0, 1)]
+            stacked = jnp.concatenate([
+                jnp.concatenate([rights[first[0]], none], axis=1),
+                jnp.concatenate([none, rights[first[1]]], axis=1)], axis=0)
+            both = dot_nn(lefts[0, second[0], :, 0:64] + lefts[1, second[1], :, 0:64], stacked)
+            for n in (0, 1):
+                close = jnp.maximum(both[:, n * TILE : (n + 1) * TILE], 0.0)
+                gained = (close * close) * (across[second[n]] - own_temp[pl.ds(first[n], 1), :])
+                at = pl.multiple_of((number + n) * 8, 8)
+                partial[pl.ds(at, 8), :] = jnp.sum(gained.reshape(TILE // 8, 8, TILE), axis=0)
         return 0
 
-    pairs = codes.shape[0]
+    pairs = codes.shape[1]
     lax.fori_loop(0, pairs // UNROLL, pair_group, 0)
     summed = partial[pl.ds(0, pairs, stride=8), :]
     for s in range(1, 8):
         summed = summed + partial[pl.ds(s, pairs, stride=8), :]
-    code_row = row_of(code_rows)
+    code_row = code_rows[0:1, :]
     number = lax.broadcasted_iota(I32, code_row.shape, 1)
-    first = jnp.where(number < count[0], lax.shift_right_logical(code_row, 5) & (tiles - 1), -1)
+    first = jnp.where(number < count[0], code_row & (tiles - 1), -1)
     firsts = onehot(tiles, first)
     gain = jnp.zeros((tiles, TILE), F32)
     for part in split3(summed):
@@ -301,7 +327,11 @@
                 beside = src[l, zt, TOP : TOP + rows, :] + src[l + 2, zt, TOP : TOP + rows, :]
                 beside = beside + (src[l + 1, zt, LOW : LOW + rows, :] + src[l + 1, zt, TOP + 1 : TOP + 1 + rows, :])
                 beside = beside + (along[zt] + end)
-                dst[l + 1, zt, TOP : TOP + rows, :] = src[l + 1, zt, TOP : TOP + rows, :] + coefs[l, zt] * beside
+                value = src[l + 1, zt, TOP : TOP + rows, :] + coefs[l, zt] * beside
+                if dst is None:
+                    out[l, :, zt * TILE : (zt + 1) * TILE] = value
+                else:
+                    dst[l + 1, zt, TOP : TOP + rows, :] = value
             return 0
 
         lax.fori_loop(0, deep, layer, 0, unroll=4)
@@ -336,28 +366,27 @@
 
         lax.fori_loop(0, CHUNKS, chunk, 0)
 
-    def stores(c):
-        at = pl.ds(c * deep, deep)
-        return [pltpu.make_async_copy(
-            cur.at[pl.ds(1 + c * deep, deep), zt, pl.ds(TOP, rows), :], out.at[at, :, pl.ds(zt * TILE, TILE)],
-            out_sem.at[c, zt]) for zt in range(blocks)]
-
     step(0)
 
     own.wait()
     first_trip.wait_recv()
-    turned = recv[...].T
-    for s in range(SLOTS):
-        code = turned[SLOTS + s : SLOTS + s + 1, :].astype(I32)
-        flux = turned[s : s + 1, :] * (1.0 / SUBSTEPS)
-        at = pl.ds(s * devices, devices)
-        hot[:, at] = onehot(hot.shape[0], plate_row(code))
-        low = onehot(TILE, code & (TILE - 1), F32)
-        for k, part in enumerate(split3(flux)):
-            lows[k, :, at] = (low * part).astype(BF16)
-    total = dot_nt(hot[...], lows[0])
-    total = total + dot_nt(hot[...], lows[1])
-    source[...] = total + dot_nt(hot[...], lows[2])
+    turned[...] = recv[...].T
+
+    def place_slot(n, _):
+        for k in range(4):
+            s = n * 4 + k
+            code = turned[pl.ds(SLOTS + s, 1), :].astype(I32)
+            flux = turned[pl.ds(s, 1), :] * (1.0 / SUBSTEPS)
+            at = pl.ds(pl.multiple_of(s * devices, TILE), devices)
+            hot[:, at] = onehot(hot.shape[0], plate_row(code))
+            low = onehot(TILE, code & (TILE - 1), F32)
+            for m, part in enumerate(split2(flux)):
+                lows[m * TILE : (m + 1) * TILE, at] = (low * part).astype(BF16)
+        return 0
+
+    lax.fori_loop(0, SLOTS // 4, place_slot, 0, unroll=2)
+    total = dot_nt(hot[...], lows[...])
+    source[...] = total[:, :TILE] + total[:, TILE:]
     heat_top(nxt)
     launch(1, 0)
 
@@ -367,22 +396,29 @@
     last = SUBSTEPS - 1
     arrive(last, 0)
     drain(last - 1, 0)
-    advance(nxt, cur, 0)
-    heat_top(cur)
-    for store in stores(0):
-        store.start()
-    flat = jnp.concatenate([cur[1, zt, TOP : TOP + rows, :] for zt in range(blocks)], axis=0)
+    advance(nxt, None, 0)
+    for zt in range(blocks):
+        out[0, :, zt * TILE : (zt + 1) * TILE] += source[zt * rows : (zt + 1) * rows, :]
+    flat = jnp.concatenate([out[0, :, zt * TILE : (zt + 1) * TILE] for zt in range(blocks)], axis=0)
     wide = jnp.concatenate([flat[k : k + TILE, :].T for k in range(0, flat.shape[0], TILE)], axis=1)
-    parts = [part.astype(BF16) for part in split3(wide)]
-    found_rows = []
-    for s in range(SLOTS):
-        at = pl.ds(s * devices, devices)
-        found = sum(dot_nn(part, hot[:, at]) for part in parts)
-        code = turned[SLOTS + s : SLOTS + s + 1, :].astype(I32)
-        low = lax.broadcasted_iota(I32, found.shape, 0) == jnp.broadcast_to(code & (TILE - 1), found.shape)
-        found_rows.append(jnp.sum(jnp.where(low, found, 0.0), axis=0, keepdims=True))
-    found_rows.append(jnp.zeros((TILE - SLOTS, devices), F32))
-    values[...] = jnp.concatenate(found_rows, axis=0).T
+    parts = jnp.concatenate(split2(wide), axis=0).astype(BF16)
+
+    def pick_slots(n, _):
+        for k in range(2):
+            at = pl.ds(pl.multiple_of((n * 2 + k) * 2 * devices, TILE), 2 * devices)
+            found = dot_nn(parts, hot[:, at])
+            found = found[:TILE] + found[TILE:]
+            s = n * 4 + k * 2
+            code = jnp.concatenate([turned[pl.ds(SLOTS + s + m, 1), :] for m in (0, 1)], axis=1).astype(I32)
+            low = lax.broadcasted_iota(I32, found.shape, 0) == jnp.broadcast_to(code & (TILE - 1), found.shape)
+            value = jnp.sum(jnp.where(low, found, 0.0), axis=0, keepdims=True)
+            for m in (0, 1):
+                found_rows[pl.ds(s + m, 1), :] = value[:, m * devices : (m + 1) * devices]
+        return 0
+
+    found_rows[...] = jnp.zeros(found_rows.shape, F32)
+    lax.fori_loop(0, SLOTS // 4, pick_slots, 0, unroll=2)
+    values[...] = found_rows[...].T
     own = pltpu.make_async_copy(values.at[pl.ds(me, 1)], back.at[pl.ds(me, 1)], own_sem.at[1])
     own.start()
     last_trip = spread_out(values, back, last_send, last_recv)
@@ -390,9 +426,7 @@
     def closing(c, _):
         arrive(last, c)
         drain(last - 1, c)
-        advance(nxt, cur, c)
-        for store in stores(c):
-            store.start()
+        advance(nxt, None, c)
         return 0
 
     lax.fori_loop(1, CHUNKS, closing, 0)
@@ -412,9 +446,6 @@
     last_trip.wait_send()
     for c in range(CHUNKS):
         drain(last, c)
-    for c in range(CHUNKS):
-        for store in stores(c):
-            store.wait()
 
 
 def call_step(codes, count, own_pos, own_temp, which, owner, cell, seen, temp, coef, fluids, subs):
@@ -428,25 +459,37 @@
         functools.partial(step_kernel, fluids, subs),
         out_shape=(
             jax.ShapeDtypeStruct(own_temp.shape, F32),
-            jax.ShapeDtypeStruct(temp.shape, F32),
+            pltpu.VMEM(temp.shape, F32),
             jax.ShapeDtypeStruct(owner.shape, F32),
         ),
-        in_specs=[SMEM_SPEC] + [VMEM_SPEC] * 3 + [SMEM_SPEC] + [VMEM_SPEC] * 4 + [ANY_SPEC] * 2,
-        out_specs=(VMEM_SPEC, ANY_SPEC, VMEM_SPEC),
+        in_specs=[SMEM_SPEC] + [HBM_SPEC] * 9,
+        out_specs=(VMEM_SPEC,) * 3,
         scratch_shapes=[
+            pltpu.SMEM(codes.shape, I32),
+            pltpu.VMEM(codes.shape, I32),
+            pltpu.VMEM(own_pos.shape, F32),
+            pltpu.VMEM(own_temp.shape, F32),
+            pltpu.VMEM(which.shape, I32),
+            pltpu.VMEM(owner.shape, I32),
+            pltpu.VMEM(cell.shape, I32),
+            pltpu.VMEM(seen.shape, F32),
+            DMA((8,)),
             pltpu.VMEM((32, wide), F32),
             pltpu.VMEM((32, wide), F32),
-            pltpu.VMEM((2 * tiles, TILE, 32), BF16),
-            pltpu.VMEM((tiles, 32, 2 * TILE), BF16),
-            pltpu.VMEM((codes.shape[0] * 8, TILE), F32),
+            pltpu.VMEM((2, 2 * tiles, TILE, TILE), BF16),
+            pltpu.VMEM((2 * tiles, TILE, TILE), F32),
+            pltpu.VMEM((tiles, 32, TILE), BF16),
+            pltpu.VMEM((codes.shape[1] * 8, TILE), F32),
             pltpu.VMEM(own_pos.shape, F32),
             pltpu.VMEM(own_temp.shape, F32),
             pltpu.VMEM((devices, ghosts), BF16),
             pltpu.VMEM((1, ghosts), F32),
             pltpu.VMEM((devices, TILE), F32),
             pltpu.VMEM((devices, TILE), F32),
+            pltpu.VMEM((TILE, devices), F32),
+            pltpu.VMEM((TILE, devices), F32),
             pltpu.VMEM((rows * blocks, devices * SLOTS), BF16),
-            pltpu.VMEM((3, TILE, devices * SLOTS), BF16),
+            pltpu.VMEM((2 * TILE, devices * SLOTS), BF16),
             pltpu.VMEM((rows * blocks, TILE), F32),
             pltpu.VMEM((devices, TILE), F32),
             pltpu.VMEM((devices, TILE), F32),
@@ -462,18 +505,18 @@
             DMA,
             DMA((2,)),
             DMA((2, blocks)),
-            DMA((CHUNKS, blocks)),
             DMA((SUBSTEPS, 2, CHUNKS)),
             DMA((SUBSTEPS, 2, CHUNKS)),
         ],
-        compiler_params=pltpu.CompilerParams(collective_id=0, has_side_effects=True, vmem_limit_bytes=60 << 20),
+        compiler_params=pltpu.CompilerParams(collective_id=0, has_side_effects=True, vmem_limit_bytes=48 << 20),
         name="step",
-    )(codes, own_pos, own_temp, codes.reshape(-1, TILE), count, which, owner, cell, seen, temp, coef)
+    )(count, *[pltpu.with_memory_space_constraint(x, pltpu.HBM) for x in (
+        codes, own_pos, own_temp, which, owner, cell, seen, temp, coef)])
 
 
 def on_device(positions, particle_temp, pair_list, pair_count, ghost_particle, ghost_owner, ghost_cell,
               wall_seen, solid_temp, conduct):
-    codes = pair_list[:, 0] * 32 + pair_list[:, 1]
+    codes = pair_list.T
 
     def tiled(x):
         return x.reshape(-1, TILE)

time: 80.7 us -> 69.7 us (0.86)
  Pallas kernels: 71.2 us -> 65.1 us
  local copies, waits for them, and re-layouts: 6.61 us -> 3.21 us
  other arithmetic: 1.32 us -> 0 us
    pallas_call x1, Pallas kernels: 71.2 us -> 65.1 us  [call_step(): pl.pallas_call(functools.partial(step_kernel, fluids, subs), out_shape=(j...]
    unnamed x5 -> x3, local copies, waits for them, and re-layouts: 6.61 us -> 3.21 us
    add x1 -> x0, other arithmetic: 1.32 us -> none  [on_device(): codes = pair_list[:, 0] * 32 + pair_list[:, 1]]
where the time goes in v3:
time: 69.7 us; the launch traced here: 69.6 us
  Pallas kernels  65.1 us (93%)
  local copies, waits for them, and re-layouts  3.21 us (5%)
  between operations  1.29 us (2%)
    pallas_call x1, Pallas kernels, call_step(): pl.pallas_call(functools.partial(step_kernel, fluids, subs), out_shape=(j...  65.1 us
    unnamed x3, local copies, waits for them, and re-layouts  3.21 us

profile of v3, /device:TPU:1, one launch (start us, length us, event | category | flops | bytes accessed | tf_op | source)
XLA Modules:
  0.0 69.6 jit_solution(16812408870953104160)
XLA Ops:
  1.3 65.1 %step.1 = (f32[16,128]{1,0:T(8,128)S(1)}, f32[32,16,2048]{2,1,0:T(8,128)S(1)}, f32[16,128]{1,0:T(8,128)S(1)}) custom-call(s32[1]{0:T(128)S(6)} %copy.17.count, s32[2,256]{1,0:T(2,128)} %bitcast.15, f32[3,2048]{1,0:T(4,128)} %pos_in.1, f32[16,128]{1,0:T(8,128)} %bitcast.10, s32[16,128]{1,0:T(8,128)} %bitcast.11, s32[16,128]{1,0:T(8,128)} %bitcast.12, ...), custom_call_target="tpu_custom_call" | custom-call | tf_op jit(solution)/shard_map/step/pallas_call | solution.py:458
  66.4 2.0 %copy.16 = f32[32,16,2048]{2,1,0:T(8,128)} copy(f32[32,16,2048]{2,1,0:T(8,128)S(1)} %get-tuple-element.10) | data formatting | bytes 8388608
  68.4 0.6 copy.18
  69.0 0.6 copy.19

commit v4 on v3

--- a/solution.py
+++ b/solution.py
@@ -12,8 +12,9 @@
 SLOTS = 32
 HEAT_RATE = 0.004
 WALL_HEAT = 0.5
-UNROLL = 16
-CHUNKS = 4
+UNROLL = 32
+CHUNKS = 8
+EARLY = 3
 AXES = ("fluid", "sub")
 VMEM_SPEC = pl.BlockSpec(memory_space=pltpu.VMEM)
 SMEM_SPEC = pl.BlockSpec(memory_space=pltpu.SMEM)
@@ -126,7 +127,7 @@
     heated, out, ghost_out,
     codes, code_rows, own_pos, own_temp, which, owner, cell, seen, small_sem,
     left, right, lefts, across, rights, partial, near_pos, near_temp, owners, rank_row, send, recv, turned, found_rows, hot, lows, source,
-    values, back, cur, nxt, coefs, weights,
+    values, back, cur, nxt, coefs, weights, wide_source, wide_coefs, resp, resp_next, side_send, side_recv,
     near_send, near_recv, first_send, first_recv, last_send, last_recv, own_sem, load_sem, send_sem, recv_sem,
 ):
     devices = fluids * subs
@@ -177,9 +178,15 @@
             for zt in range(blocks):
                 buf[l, zt, TOP : TOP + rows, :] = jnp.zeros((rows, TILE), F32)
 
-    for edge, x in ((0, LOW), (devices - 1, TOP + rows)):
+    for buf in (resp, resp_next):
+        buf[...] = jnp.zeros(buf.shape, F32)
+
+    for edge, x, far in ((0, LOW, 0), (devices - 1, TOP + rows, rows + 8)):
         @pl.when(me == edge)
         def _():
+            wide_source[:, far : far + 8, :] = jnp.zeros((blocks, 8, TILE), F32)
+            wide_coefs[:, :, far : far + 8, :] = jnp.zeros((EARLY, blocks, 8, TILE), F32)
+
             def wipe(l, _):
                 for buf in (cur, nxt):
                     for zt in range(blocks):
@@ -220,6 +227,16 @@
 
     def drain(k, c):
         each(lambda side: halo(k, side, c).wait_send())
+
+    def side_copy(n, side):
+        at, to = ((pl.ds(0, 8), pl.ds(rows + 8, 8)), (pl.ds(rows - 8, 8), pl.ds(0, 8)))[side]
+        if n == 0:
+            src, dst = coefs.at[pl.ds(0, EARLY), :, at, :], wide_coefs.at[:, :, to, :]
+        else:
+            src, dst = source.at[:, at, :], wide_source.at[:, to, :]
+        return pltpu.make_async_remote_copy(
+            src_ref=src, dst_ref=dst, send_sem=side_send.at[n, side], recv_sem=side_recv.at[n, 1 - side],
+            device_id=place(me - 1 if side == 0 else me + 1), device_id_type=MESH)
 
     pl.semaphore_wait(barrier, devices - 1)
     behind = (fluid, lax.rem(sub + subs - 1, subs))
@@ -232,79 +249,12 @@
         load.wait()
     for c in range(CHUNKS):
         launch(0, c)
-
-    owners[...] = onehot(devices, row_of(owner))
-    rank_row[...] = ranks(owners[...], devices)
-
-    for copy in near:
-        copy.wait_recv()
-    put_features(near_pos[...], row_of(near_temp), left, None)
-    for t in range(tiles):
-        put_tile(left, t, tiles + t, lefts, across)
-
-    none = jnp.zeros((32, TILE), BF16)
-
-    def pair_group(group, _):
-        for k in range(0, UNROLL, 2):
-            number = group * UNROLL + k
-            first = [codes[0, number + n] & (tiles - 1) for n in (0, 1)]
-            second = [codes[1, number + n] & (2 * tiles - 1) for n in (0, 1)]
-            stacked = jnp.concatenate([
-                jnp.concatenate([rights[first[0]], none], axis=1),
-                jnp.concatenate([none, rights[first[1]]], axis=1)], axis=0)
-            both = dot_nn(lefts[0, second[0], :, 0:64] + lefts[1, second[1], :, 0:64], stacked)
-            for n in (0, 1):
-                close = jnp.maximum(both[:, n * TILE : (n + 1) * TILE], 0.0)
-                gained = (close * close) * (across[second[n]] - own_temp[pl.ds(first[n], 1), :])
-                at = pl.multiple_of((number + n) * 8, 8)
-                partial[pl.ds(at, 8), :] = jnp.sum(gained.reshape(TILE // 8, 8, TILE), axis=0)
-        return 0
-
-    pairs = codes.shape[1]
-    lax.fori_loop(0, pairs // UNROLL, pair_group, 0)
-    summed = partial[pl.ds(0, pairs, stride=8), :]
-    for s in range(1, 8):
-        summed = summed + partial[pl.ds(s, pairs, stride=8), :]
-    code_row = code_rows[0:1, :]
-    number = lax.broadcasted_iota(I32, code_row.shape, 1)
-    first = jnp.where(number < count[0], code_row & (tiles - 1), -1)
-    firsts = onehot(tiles, first)
-    gain = jnp.zeros((tiles, TILE), F32)
-    for part in split3(summed):
-        gain = gain + dot_nn(firsts, part.astype(BF16))
-    out_temp = own_temp[...] + HEAT_RATE * gain
-    heated[...] = out_temp
-
-    parts = jnp.concatenate(split3(out_temp), axis=0).T.astype(BF16)
-    which_row = row_of(which)
-    high = onehot(tiles, lax.shift_right_logical(which_row, 7))
-    picked = dot_nn(parts, jnp.concatenate([high] * 3, axis=0))
-    low = jnp.broadcast_to(which_row & (TILE - 1), picked.shape)
-    hit = lax.broadcasted_iota(I32, picked.shape, 0) == low
-    flux = WALL_HEAT * (jnp.sum(jnp.where(hit, picked, 0.0), axis=0, keepdims=True) - row_of(seen))
-    slot = onehot(SLOTS, rank_row[...].astype(I32), F32)
-    cell_row = row_of(cell)
-    cells = ((cell_row & ~255).astype(F32), (cell_row & 255).astype(F32), None)
-    total = jnp.zeros((devices, 2 * SLOTS), F32)
-    for f, c in zip(split3(flux), cells):
-        lower_half = jnp.zeros_like(slot) if c is None else slot * c
-        total = total + dot_nt(owners[...], jnp.concatenate([slot * f, lower_half], axis=0).astype(BF16))
-    send[...] = jnp.concatenate([total, jnp.zeros((devices, TILE - 2 * SLOTS), F32)], axis=1)
-
-    def spread_out(src, dst, sends, recvs):
-        everyone(lambda f, s: pltpu.make_async_remote_copy(
-            src_ref=src.at[pl.ds(f * subs + s, 1)], dst_ref=dst.at[pl.ds(me, 1)], send_sem=sends, recv_sem=recvs,
-            device_id=(f, s), device_id_type=MESH).start())
-        return pltpu.make_async_remote_copy(
-            src_ref=src.at[pl.ds(0, devices - 1)], dst_ref=dst.at[pl.ds(0, devices - 1)], send_sem=sends,
-            recv_sem=recvs, device_id=behind, device_id_type=MESH)
-
-    own = pltpu.make_async_copy(send.at[pl.ds(me, 1)], recv.at[pl.ds(me, 1)], own_sem.at[0])
-    own.start()
-    first_trip = spread_out(send, recv, first_send, first_recv)
-
     for load in loads[blocks:]:
         load.wait()
+    each(lambda side: side_copy(0, side).start())
+    for l in range(EARLY):
+        wide_coefs[l, :, 8 : 8 + rows, :] = coefs[l]
+
     lane = lax.broadcasted_iota(I32, (rows, TILE), 1)
     lower = lane < TILE // 2
 
@@ -338,35 +288,126 @@
 
     def heat_top(dst):
         for zt in range(blocks):
-            dst[1, zt, TOP : TOP + rows, :] += source[zt * rows : (zt + 1) * rows, :]
+            dst[1, zt, TOP : TOP + rows, :] += source[zt]
 
     def step(k):
         src, dst = (cur, nxt) if k % 2 == 0 else (nxt, cur)
 
         def chunk(c, _):
-            arrive(k, c)
-            if k > 0:
+            def ready():
+                arrive(k, c)
+                if k > 0:
+                    drain(k - 1, c)
+
+            if k == EARLY:
+                pl.when(c > 0)(lambda: arrive(k, c))
                 drain(k - 1, c)
+            elif k == EARLY + 1:
+                arrive(k, c)
+                pl.when(c > 0)(lambda: drain(k - 1, c))
+            else:
+                ready()
             advance(src, dst, c)
-            if k == 0:
-                @pl.when(c > 0)
-                def _():
-                    launch(1, c)
-            elif k + 1 < SUBSTEPS:
-                @pl.when(c == 0)
-                def _():
-                    heat_top(dst)
-
-                launch(k + 1, c)
-            else:
-                @pl.when(c == 0)
-                def _():
-                    heat_top(dst)
+            if k >= EARLY:
+                pl.when(c == 0)(lambda: heat_top(dst))
+            launch(k + 1, c)
             return 0
 
         lax.fori_loop(0, CHUNKS, chunk, 0)
 
+    def respond(src, dst, layers_now):
+        high_rows = rows + 16
+        for l in range(layers_now):
+            center = [src[l + 1, zt, 8 : 8 + high_rows, :] for zt in range(blocks)]
+            high = [x.astype(BF16) for x in center]
+            low = [(x - y.astype(F32)).astype(BF16) for x, y in zip(center, high)]
+            both = jnp.concatenate([jnp.concatenate(high, axis=0), jnp.concatenate(low, axis=0)], axis=1)
+            both = dot_nn(both, weights[...])
+            part = [both[zt * high_rows : (zt + 1) * high_rows, :] for zt in range(blocks)]
+            nothing = jnp.zeros((high_rows, TILE), F32)
+            left_lanes = lax.broadcasted_iota(I32, nothing.shape, 1) < TILE // 2
+            for zt in range(blocks):
+                end = jnp.where(left_lanes, part[zt - 1][:, TILE:] if zt > 0 else nothing,
+                                part[zt + 1][:, TILE:] if zt + 1 < blocks else nothing)
+                beside = src[l, zt, 8 : 8 + high_rows, :] + src[l + 2, zt, 8 : 8 + high_rows, :]
+                beside = beside + (src[l + 1, zt, 7 : 7 + high_rows, :] + src[l + 1, zt, 9 : 9 + high_rows, :])
+                beside = beside + (part[zt][:, :TILE] + end)
+                value = src[l + 1, zt, 8 : 8 + high_rows, :] + wide_coefs[l, zt] * beside
+                dst[l + 1, zt, 8 : 8 + high_rows, :] = value + wide_source[zt] if l == 0 else value
+
+    owners[...] = onehot(devices, row_of(owner))
+    rank_row[...] = ranks(owners[...], devices)
+
+    for copy in near:
+        copy.wait_recv()
+    put_features(near_pos[...], row_of(near_temp), left, None)
+    for t in range(tiles):
+        put_tile(left, t, tiles + t, lefts, across)
+
+    none = jnp.zeros((32, TILE), BF16)
+
+    def pair_group(group, _):
+        for k in range(0, UNROLL, 2):
+            number = group * UNROLL + k
+            first = [codes[0, number + n] & (tiles - 1) for n in (0, 1)]
+            second = [codes[1, number + n] & (2 * tiles - 1) for n in (0, 1)]
+            stacked = jnp.concatenate([
+                jnp.concatenate([rights[first[0]], none], axis=1),
+                jnp.concatenate([none, rights[first[1]]], axis=1)], axis=0)
+            both = dot_nn(lefts[0, second[0], :, 0:64] + lefts[1, second[1], :, 0:64], stacked)
+            for n in (0, 1):
+                close = jnp.maximum(both[:, n * TILE : (n + 1) * TILE], 0.0)
+                gained = (close * close) * (across[second[n]] - own_temp[pl.ds(first[n], 1), :])
+                at = pl.multiple_of((number + n) * 8, 8)
+                partial[pl.ds(at, 8), :] = jnp.sum(gained.reshape(TILE // 8, 8, TILE), axis=0)
+        return 0
+
+    pairs = codes.shape[1]
+    lax.fori_loop(0, pairs // UNROLL // 2, pair_group, 0)
     step(0)
+    lax.fori_loop(pairs // UNROLL // 2, pairs // UNROLL, pair_group, 0)
+    summed = partial[pl.ds(0, pairs, stride=8), :]
+    for s in range(1, 8):
+        summed = summed + partial[pl.ds(s, pairs, stride=8), :]
+    code_row = code_rows[0:1, :]
+    number = lax.broadcasted_iota(I32, code_row.shape, 1)
+    first = jnp.where(number < count[0], code_row & (tiles - 1), -1)
+    firsts = onehot(tiles, first)
+    gain = jnp.zeros((tiles, TILE), F32)
+    for part in split3(summed):
+        gain = gain + dot_nn(firsts, part.astype(BF16))
+    out_temp = own_temp[...] + HEAT_RATE * gain
+    heated[...] = out_temp
+
+    parts = jnp.concatenate(split3(out_temp), axis=0).T.astype(BF16)
+    which_row = row_of(which)
+    high = onehot(tiles, lax.shift_right_logical(which_row, 7))
+    picked = dot_nn(parts, jnp.concatenate([high] * 3, axis=0))
+    low = jnp.broadcast_to(which_row & (TILE - 1), picked.shape)
+    hit = lax.broadcasted_iota(I32, picked.shape, 0) == low
+    flux = WALL_HEAT * (jnp.sum(jnp.where(hit, picked, 0.0), axis=0, keepdims=True) - row_of(seen))
+    slot = onehot(SLOTS, rank_row[...].astype(I32), F32)
+    cell_row = row_of(cell)
+    cells = ((cell_row & ~255).astype(F32), (cell_row & 255).astype(F32), None)
+    total = jnp.zeros((devices, 2 * SLOTS), F32)
+    for f, c in zip(split3(flux), cells):
+        lower_half = jnp.zeros_like(slot) if c is None else slot * c
+        total = total + dot_nt(owners[...], jnp.concatenate([slot * f, lower_half], axis=0).astype(BF16))
+    send[...] = jnp.concatenate([total, jnp.zeros((devices, TILE - 2 * SLOTS), F32)], axis=1)
+
+    def spread_out(src, dst, sends, recvs):
+        everyone(lambda f, s: pltpu.make_async_remote_copy(
+            src_ref=src.at[pl.ds(f * subs + s, 1)], dst_ref=dst.at[pl.ds(me, 1)], send_sem=sends, recv_sem=recvs,
+            device_id=(f, s), device_id_type=MESH).start())
+        return pltpu.make_async_remote_copy(
+            src_ref=src.at[pl.ds(0, devices - 1)], dst_ref=dst.at[pl.ds(0, devices - 1)], send_sem=sends,
+            recv_sem=recvs, device_id=behind, device_id_type=MESH)
+
+    own = pltpu.make_async_copy(send.at[pl.ds(me, 1)], recv.at[pl.ds(me, 1)], own_sem.at[0])
+    own.start()
+    first_trip = spread_out(send, recv, first_send, first_recv)
+
+    step(1)
 
     own.wait()
     first_trip.wait_recv()
@@ -386,11 +427,31 @@
 
     lax.fori_loop(0, SLOTS // 4, place_slot, 0, unroll=2)
     total = dot_nt(hot[...], lows[...])
-    source[...] = total[:, :TILE] + total[:, TILE:]
-    heat_top(nxt)
-    launch(1, 0)
-
-    for k in range(1, SUBSTEPS - 1):
+    total = total[:, :TILE] + total[:, TILE:]
+    for zt in range(blocks):
+        source[zt] = total[zt * rows : (zt + 1) * rows, :]
+        wide_source[zt, 8 : 8 + rows, :] = total[zt * rows : (zt + 1) * rows, :]
+    each(lambda side: side_copy(1, side).start())
+    step(2)
+
+    for n in (0, 1):
+        each(lambda side: side_copy(n, 1 - side).wait_recv())
+    for zt in range(blocks):
+        resp[1, zt, 8 : 24 + rows, :] = wide_source[zt]
+    pair = (resp, resp_next)
+    for k in range(2, EARLY + 1):
+        respond(pair[k % 2], pair[(k + 1) % 2], k)
+    done = pair[(EARLY + 1) % 2]
+    target = (cur, nxt)[EARLY % 2]
+    arrive(EARLY, 0)
+    drain(EARLY, 0)
+    for l in range(EARLY):
+        for zt in range(blocks):
+            target[l + 1, zt, TOP : TOP + rows, :] += done[l + 1, zt, 16 : 16 + rows, :]
+            target[l + 1, zt, LOW : LOW + 1, :] += done[l + 1, zt, 15:16, :]
+            target[l + 1, zt, TOP + rows : TOP + rows + 1, :] += done[l + 1, zt, 16 + rows : 17 + rows, :]
+
+    for k in range(EARLY, SUBSTEPS - 1):
         step(k)
 
     last = SUBSTEPS - 1
@@ -398,7 +459,7 @@
     drain(last - 1, 0)
     advance(nxt, None, 0)
     for zt in range(blocks):
-        out[0, :, zt * TILE : (zt + 1) * TILE] += source[zt * rows : (zt + 1) * rows, :]
+        out[0, :, zt * TILE : (zt + 1) * TILE] += source[zt]
     flat = jnp.concatenate([out[0, :, zt * TILE : (zt + 1) * TILE] for zt in range(blocks)], axis=0)
     wide = jnp.concatenate([flat[k : k + TILE, :].T for k in range(0, flat.shape[0], TILE)], axis=1)
     parts = jnp.concatenate(split2(wide), axis=0).astype(BF16)
@@ -446,6 +507,8 @@
     last_trip.wait_send()
     for c in range(CHUNKS):
         drain(last, c)
+    for n in (0, 1):
+        each(lambda side: side_copy(n, side).wait_send())
 
 
 def call_step(codes, count, own_pos, own_temp, which, owner, cell, seen, temp, coef, fluids, subs):
@@ -490,13 +553,19 @@
             pltpu.VMEM((TILE, devices), F32),
             pltpu.VMEM((rows * blocks, devices * SLOTS), BF16),
             pltpu.VMEM((2 * TILE, devices * SLOTS), BF16),
-            pltpu.VMEM((rows * blocks, TILE), F32),
+            pltpu.VMEM((blocks, rows, TILE), F32),
             pltpu.VMEM((devices, TILE), F32),
             pltpu.VMEM((devices, TILE), F32),
             pltpu.VMEM((layers + 2, blocks, TOP + rows + 8, TILE), F32),
             pltpu.VMEM((layers + 2, blocks, TOP + rows + 8, TILE), F32),
             pltpu.VMEM((layers, blocks, rows, TILE), F32),
             pltpu.VMEM((2 * TILE, 2 * TILE), BF16),
+            pltpu.VMEM((blocks, rows + 16, TILE), F32),
+            pltpu.VMEM((EARLY, blocks, rows + 16, TILE), F32),
+            pltpu.VMEM((EARLY + 2, blocks, rows + 32, TILE), F32),
+            pltpu.VMEM((EARLY + 2, blocks, rows + 32, TILE), F32),
+            DMA((2, 2)),
+            DMA((2, 2)),
             DMA((2,)),
             DMA((2,)),
             DMA,

time: 69.7 us -> 60.5 us (0.87)
  Pallas kernels: 65.1 us -> 55.9 us
    pallas_call x1, Pallas kernels: 65.1 us -> 55.9 us  [call_step(): pl.pallas_call(functools.partial(step_kernel, fluids, subs), out_shape=(j...]
where the time goes in v4:
time: 60.5 us; the launch traced here: 60.4 us
  Pallas kernels  55.9 us (92%)
  local copies, waits for them, and re-layouts  3.21 us (5%)
  between operations  1.29 us (2%)
    pallas_call x1, Pallas kernels, call_step(): pl.pallas_call(functools.partial(step_kernel, fluids, subs), out_shape=(j...  55.9 us
    unnamed x3, local copies, waits for them, and re-layouts  3.21 us

profile of v4, /device:TPU:1, one launch (start us, length us, event | category | flops | bytes accessed | tf_op | source)
XLA Modules:
  0.0 60.4 jit_solution(10242631335496620873)
XLA Ops:
  1.3 55.9 %step.1 = (f32[16,128]{1,0:T(8,128)S(1)}, f32[32,16,2048]{2,1,0:T(8,128)S(1)}, f32[16,128]{1,0:T(8,128)S(1)}) custom-call(s32[1]{0:T(128)S(6)} %copy.17.count, s32[2,256]{1,0:T(2,128)} %bitcast.15, f32[3,2048]{1,0:T(4,128)} %pos_in.1, f32[16,128]{1,0:T(8,128)} %bitcast.10, s32[16,128]{1,0:T(8,128)} %bitcast.11, s32[16,128]{1,0:T(8,128)} %bitcast.12, ...), custom_call_target="tpu_custom_call" | custom-call | tf_op jit(solution)/shard_map/step/pallas_call | solution.py:521
  57.1 2.0 %copy.16 = f32[32,16,2048]{2,1,0:T(8,128)} copy(f32[32,16,2048]{2,1,0:T(8,128)S(1)} %get-tuple-element.10) | data formatting | bytes 8388608
  59.2 0.6 copy.18
  59.8 0.6 copy.19

commit v5 on v4

--- a/solution.py
+++ b/solution.py
@@ -14,7 +14,7 @@
 WALL_HEAT = 0.5
 UNROLL = 32
 CHUNKS = 8
-EARLY = 3
+EARLY = 5
 AXES = ("fluid", "sub")
 VMEM_SPEC = pl.BlockSpec(memory_space=pltpu.VMEM)
 SMEM_SPEC = pl.BlockSpec(memory_space=pltpu.SMEM)
@@ -126,7 +126,7 @@
     fluids, subs, count, codes_in, pos_in, temp_in, which_in, owner_in, cell_in, seen_in, temp, coef,
     heated, out, ghost_out,
     codes, code_rows, own_pos, own_temp, which, owner, cell, seen, small_sem,
-    left, right, lefts, across, rights, partial, near_pos, near_temp, owners, rank_row, send, recv, turned, found_rows, hot, lows, source,
+    left, right, lefts, across, rights, partial, near_pos, near_temp, owners, slots, send, recv, turned, found_rows, hot, lows, source,
     values, back, cur, nxt, coefs, weights, wide_source, wide_coefs, resp, resp_next, side_send, side_recv,
     near_send, near_recv, first_send, first_recv, last_send, last_recv, own_sem, load_sem, send_sem, recv_sem,
 ):
@@ -142,16 +142,17 @@
         return (lax.div(index, subs), lax.rem(index, subs))
 
     def everyone(act):
+        half = fluids // 2
+
+        def row(up, _):
+            other = lax.rem(fluid + 1 + lax.rem(up + half, fluids - 1), fluids)
+            for by in range(subs):
+                act(other, lax.rem(sub + subs // 2 + by, subs))
+            return 0
+
+        lax.fori_loop(0, fluids - 1, row, 0)
         for by in range(1, subs):
             act(fluid, lax.rem(sub + by, subs))
-
-        def row(up, _):
-            other = lax.rem(fluid + up, fluids)
-            for by in range(subs):
-                act(other, lax.rem(sub + by, subs))
-            return 0
-
-        lax.fori_loop(1, fluids, row, 0)
 
     small = [pltpu.make_async_copy(src, dst, small_sem.at[n]) for n, (src, dst) in enumerate((
         (codes_in, codes), (codes_in, code_rows), (pos_in, own_pos), (temp_in, own_temp), (which_in, which),
@@ -286,34 +287,18 @@
 
         lax.fori_loop(0, deep, layer, 0, unroll=4)
 
-    def heat_top(dst):
-        for zt in range(blocks):
-            dst[1, zt, TOP : TOP + rows, :] += source[zt]
-
-    def step(k):
+    def step(k, first=0, end=CHUNKS):
         src, dst = (cur, nxt) if k % 2 == 0 else (nxt, cur)
 
         def chunk(c, _):
-            def ready():
-                arrive(k, c)
-                if k > 0:
-                    drain(k - 1, c)
-
-            if k == EARLY:
-                pl.when(c > 0)(lambda: arrive(k, c))
+            arrive(k, c)
+            if k > 0:
                 drain(k - 1, c)
-            elif k == EARLY + 1:
-                arrive(k, c)
-                pl.when(c > 0)(lambda: drain(k - 1, c))
-            else:
-                ready()
             advance(src, dst, c)
-            if k >= EARLY:
-                pl.when(c == 0)(lambda: heat_top(dst))
             launch(k + 1, c)
             return 0
 
-        lax.fori_loop(0, CHUNKS, chunk, 0)
+        lax.fori_loop(first, end, chunk, 0)
 
     def respond(src, dst, layers_now):
         high_rows = rows + 16
@@ -336,7 +321,7 @@
                 dst[l + 1, zt, 8 : 8 + high_rows, :] = value + wide_source[zt] if l == 0 else value
 
     owners[...] = onehot(devices, row_of(owner))
-    rank_row[...] = ranks(owners[...], devices)
+    slots[...] = onehot(SLOTS, ranks(owners[...], devices).astype(I32), F32)
 
     for copy in near:
         copy.wait_recv()
@@ -366,6 +351,7 @@
     lax.fori_loop(0, pairs // UNROLL // 2, pair_group, 0)
     step(0)
     lax.fori_loop(pairs // UNROLL // 2, pairs // UNROLL, pair_group, 0)
+    step(1)
     summed = partial[pl.ds(0, pairs, stride=8), :]
     for s in range(1, 8):
         summed = summed + partial[pl.ds(s, pairs, stride=8), :]
@@ -386,7 +372,7 @@
     low = jnp.broadcast_to(which_row & (TILE - 1), picked.shape)
     hit = lax.broadcasted_iota(I32, picked.shape, 0) == low
     flux = WALL_HEAT * (jnp.sum(jnp.where(hit, picked, 0.0), axis=0, keepdims=True) - row_of(seen))
-    slot = onehot(SLOTS, rank_row[...].astype(I32), F32)
+    slot = slots[...]
     cell_row = row_of(cell)
     cells = ((cell_row & ~255).astype(F32), (cell_row & 255).astype(F32), None)
     total = jnp.zeros((devices, 2 * SLOTS), F32)
@@ -407,7 +393,7 @@
     own.start()
     first_trip = spread_out(send, recv, first_send, first_recv)
 
-    step(1)
+    step(2)
 
     own.wait()
     first_trip.wait_recv()
@@ -432,7 +418,9 @@
         source[zt] = total[zt * rows : (zt + 1) * rows, :]
         wide_source[zt, 8 : 8 + rows, :] = total[zt * rows : (zt + 1) * rows, :]
     each(lambda side: side_copy(1, side).start())
-    step(2)
+    step(3)
+    ahead = 2
+    step(4, 0, ahead)
 
     for n in (0, 1):
         each(lambda side: side_copy(n, 1 - side).wait_recv())
@@ -443,20 +431,16 @@
         respond(pair[k % 2], pair[(k + 1) % 2], k)
     done = pair[(EARLY + 1) % 2]
     target = (cur, nxt)[EARLY % 2]
-    arrive(EARLY, 0)
-    drain(EARLY, 0)
+    for c in range(ahead):
+        arrive(EARLY, c)
+        drain(EARLY, c)
     for l in range(EARLY):
         for zt in range(blocks):
             target[l + 1, zt, TOP : TOP + rows, :] += done[l + 1, zt, 16 : 16 + rows, :]
             target[l + 1, zt, LOW : LOW + 1, :] += done[l + 1, zt, 15:16, :]
             target[l + 1, zt, TOP + rows : TOP + rows + 1, :] += done[l + 1, zt, 16 + rows : 17 + rows, :]
 
-    for k in range(EARLY, SUBSTEPS - 1):
-        step(k)
-
     last = SUBSTEPS - 1
-    arrive(last, 0)
-    drain(last - 1, 0)
     advance(nxt, None, 0)
     for zt in range(blocks):
         out[0, :, zt * TILE : (zt + 1) * TILE] += source[zt]
@@ -483,10 +467,10 @@
     own = pltpu.make_async_copy(values.at[pl.ds(me, 1)], back.at[pl.ds(me, 1)], own_sem.at[1])
     own.start()
     last_trip = spread_out(values, back, last_send, last_recv)
+    step(4, ahead, CHUNKS)
 
     def closing(c, _):
-        arrive(last, c)
-        drain(last - 1, c)
+        pl.when(c >= ahead)(lambda: arrive(last, c))
         advance(nxt, None, c)
         return 0
 
@@ -494,10 +478,8 @@
 
     own.wait()
     last_trip.wait_recv()
-    found = dot_nn(jnp.concatenate(split3(back[...].T[0:SLOTS, :]), axis=0).astype(BF16), owners[...])
-    found = found[0:SLOTS] + found[SLOTS : 2 * SLOTS] + found[2 * SLOTS :]
-    slot = onehot(SLOTS, rank_row[...].astype(I32), F32)
-    ghost = jnp.sum(found * slot, axis=0, keepdims=True)
+    found = dot_nn(jnp.concatenate(split2(back[...].T[0:SLOTS, :]), axis=0).astype(BF16), owners[...])
+    ghost = jnp.sum((found[0:SLOTS] + found[SLOTS:]) * slots[...], axis=0, keepdims=True)
     for t in range(ghost_out.shape[0]):
         ghost_out[t : t + 1, :] = ghost[:, t * TILE : (t + 1) * TILE]
 
@@ -506,7 +488,9 @@
     first_trip.wait_send()
     last_trip.wait_send()
     for c in range(CHUNKS):
-        drain(last, c)
+        drain(last - 1, c)
+        if c >= ahead:
+            drain(last, c)
     for n in (0, 1):
         each(lambda side: side_copy(n, side).wait_send())
 
@@ -521,9 +505,9 @@
     return pl.pallas_call(
         functools.partial(step_kernel, fluids, subs),
         out_shape=(
-            jax.ShapeDtypeStruct(own_temp.shape, F32),
+            pltpu.VMEM(own_temp.shape, F32),
             pltpu.VMEM(temp.shape, F32),
-            jax.ShapeDtypeStruct(owner.shape, F32),
+            pltpu.VMEM(owner.shape, F32),
         ),
         in_specs=[SMEM_SPEC] + [HBM_SPEC] * 9,
         out_specs=(VMEM_SPEC,) * 3,
@@ -546,7 +530,7 @@
             pltpu.VMEM(own_pos.shape, F32),
             pltpu.VMEM(own_temp.shape, F32),
             pltpu.VMEM((devices, ghosts), BF16),
-            pltpu.VMEM((1, ghosts), F32),
+            pltpu.VMEM((SLOTS, ghosts), F32),
             pltpu.VMEM((devices, TILE), F32),
             pltpu.VMEM((devices, TILE), F32),
             pltpu.VMEM((TILE, devices), F32),
@@ -583,6 +567,29 @@
         codes, own_pos, own_temp, which, owner, cell, seen, temp, coef)])
 
 
+def finish_kernel(plate, first, second, plate_out, first_out, second_out, sem):
+    deep = plate.shape[0] // 8
+    copies = [pltpu.make_async_copy(plate.at[pl.ds(n * deep, deep)], plate_out.at[pl.ds(n * deep, deep)], sem.at[n]) for n in range(8)]
+    copies.append(pltpu.make_async_copy(first, first_out, sem.at[8]))
+    copies.append(pltpu.make_async_copy(second, second_out, sem.at[9]))
+    for copy in copies:
+        copy.start()
+    for copy in copies:
+        copy.wait()
+
+
+def call_finish(*arrays):
+    return pl.pallas_call(
+        finish_kernel,
+        out_shape=tuple(jax.ShapeDtypeStruct(x.shape, x.dtype) for x in arrays),
+        in_specs=[VMEM_SPEC] * 3,
+        out_specs=(HBM_SPEC,) * 3,
+        scratch_shapes=[pltpu.SemaphoreType.DMA((10,))],
+        compiler_params=pltpu.CompilerParams(vmem_limit_bytes=16 << 20),
+        name="finish",
+    )(*arrays)
+
+
 def on_device(positions, particle_temp, pair_list, pair_count, ghost_particle, ghost_owner, ghost_cell,
               wall_seen, solid_temp, conduct):
     codes = pair_list.T
@@ -593,6 +600,7 @@
     heated, temp, ghost = call_step(
         codes, pair_count, positions, tiled(particle_temp), tiled(ghost_particle), tiled(ghost_owner),
         tiled(ghost_cell), tiled(wall_seen), solid_temp, conduct, lax.axis_size(AXES[0]), lax.axis_size(AXES[1]))
+    temp, heated, ghost = call_finish(temp, heated, ghost)
     return heated.reshape(-1), temp, ghost.reshape(-1)
 
 

time: 60.5 us -> 56.8 us (0.939)
  local copies, waits for them, and re-layouts: 3.21 us -> 0 us
    unnamed x3 -> x0, local copies, waits for them, and re-layouts: 3.21 us -> none
    pallas_call x1 -> x2, Pallas kernels: 55.9 us -> 55.3 us  [the longest x1 53.2 us: call_step(): pl.pallas_call(functools.partial(step_kernel, fluids, subs), out_shape=(p...]
where the time goes in v5:
time: 56.8 us; the launch traced here: 56.6 us
  Pallas kernels  55.3 us (97%)
  between operations  1.29 us (2%)
    pallas_call x1, Pallas kernels, call_step(): pl.pallas_call(functools.partial(step_kernel, fluids, subs), out_shape=(p...  53.2 us
    pallas_call x1, Pallas kernels, call_finish(): pl.pallas_call(finish_kernel, out_shape=tuple((jax.ShapeDtypeStruct(x.sha...  2.09 us

profile of v5, /device:TPU:1, one launch (start us, length us, event | category | flops | bytes accessed | tf_op | source)
XLA Modules:
  0.0 56.6 jit_solution(16311539018254739612)
XLA Ops:
  1.3 53.2 %step.1 = (f32[16,128]{1,0:T(8,128)S(1)}, f32[32,16,2048]{2,1,0:T(8,128)S(1)}, f32[16,128]{1,0:T(8,128)S(1)}) custom-call(s32[1]{0:T(128)S(6)} %copy.13.count, s32[2,256]{1,0:T(2,128)} %bitcast.13, f32[3,2048]{1,0:T(4,128)} %pos_in.1, f32[16,128]{1,0:T(8,128)} %bitcast.8, s32[16,128]{1,0:T(8,128)} %bitcast.9, s32[16,128]{1,0:T(8,128)} %bitcast.10, ...), custom_call_target="tpu_custom_call" | custom-call | tf_op jit(solution)/shard_map/step/pallas_call | solution.py:505
  54.5 2.1 %finish.1 = (f32[32,16,2048]{2,1,0:T(8,128)}, f32[16,128]{1,0:T(8,128)}, f32[16,128]{1,0:T(8,128)}) custom-call(f32[32,16,2048]{2,1,0:T(8,128)S(1)} %get-tuple-element.9.plate, f32[16,128]{1,0:T(8,128)S(1)} %get-tuple-element.10.first, f32[16,128]{1,0:T(8,128)S(1)} %get-tuple-element.11.second), custom_call_target="tpu_custom_call" | custom-call | tf_op jit(solution)/shard_map/finish/pallas_call | solution.py:582

commit v6 on v5

--- a/solution.py
+++ b/solution.py
@@ -301,13 +301,12 @@
         lax.fori_loop(first, end, chunk, 0)
 
     def respond(src, dst, layers_now):
-        high_rows = rows + 16
-        for l in range(layers_now):
-            center = [src[l + 1, zt, 8 : 8 + high_rows, :] for zt in range(blocks)]
-            high = [x.astype(BF16) for x in center]
-            low = [(x - y.astype(F32)).astype(BF16) for x, y in zip(center, high)]
-            both = jnp.concatenate([jnp.concatenate(high, axis=0), jnp.concatenate(low, axis=0)], axis=1)
-            both = dot_nn(both, weights[...])
+        high_rows = rows + 8
+        def layer(l, _):
+            center = jnp.concatenate([src[l + 1, zt, 8 : 8 + high_rows, :] for zt in range(blocks)], axis=0)
+            high = center.astype(BF16)
+            low = (center - high.astype(F32)).astype(BF16)
+            both = dot_nn(jnp.concatenate([high, low], axis=1), weights[...])
             part = [both[zt * high_rows : (zt + 1) * high_rows, :] for zt in range(blocks)]
             nothing = jnp.zeros((high_rows, TILE), F32)
             left_lanes = lax.broadcasted_iota(I32, nothing.shape, 1) < TILE // 2
@@ -317,8 +316,13 @@
                 beside = src[l, zt, 8 : 8 + high_rows, :] + src[l + 2, zt, 8 : 8 + high_rows, :]
                 beside = beside + (src[l + 1, zt, 7 : 7 + high_rows, :] + src[l + 1, zt, 9 : 9 + high_rows, :])
                 beside = beside + (part[zt][:, :TILE] + end)
-                value = src[l + 1, zt, 8 : 8 + high_rows, :] + wide_coefs[l, zt] * beside
-                dst[l + 1, zt, 8 : 8 + high_rows, :] = value + wide_source[zt] if l == 0 else value
+                value = src[l + 1, zt, 8 : 8 + high_rows, :] + wide_coefs[l, zt, 4 : 4 + high_rows, :] * beside
+                dst[l + 1, zt, 8 : 8 + high_rows, :] = value
+            return 0
+
+        lax.fori_loop(0, layers_now, layer, 0)
+        for zt in range(blocks):
+            dst[1, zt, 8 : 8 + high_rows, :] += wide_source[zt, 4 : 4 + high_rows, :]
 
     owners[...] = onehot(devices, row_of(owner))
     slots[...] = onehot(SLOTS, ranks(owners[...], devices).astype(I32), F32)
@@ -425,20 +429,26 @@
     for n in (0, 1):
         each(lambda side: side_copy(n, 1 - side).wait_recv())
     for zt in range(blocks):
-        resp[1, zt, 8 : 24 + rows, :] = wide_source[zt]
-    pair = (resp, resp_next)
-    for k in range(2, EARLY + 1):
-        respond(pair[k % 2], pair[(k + 1) % 2], k)
-    done = pair[(EARLY + 1) % 2]
+        resp[1, zt, 8 : 16 + rows, :] = wide_source[zt, 4 : 12 + rows, :]
+        resp[1, zt, 7:8, :] = wide_source[zt, 3:4, :]
+        resp[1, zt, 16 + rows : 17 + rows, :] = wide_source[zt, 12 + rows : 13 + rows, :]
+
+    def respond_twice(n, _):
+        respond(resp, resp_next, 2 * n)
+        respond(resp_next, resp, 2 * n + 1)
+        return 0
+
+    lax.fori_loop(1, EARLY // 2 + 1, respond_twice, 0)
+    done = resp
     target = (cur, nxt)[EARLY % 2]
     for c in range(ahead):
         arrive(EARLY, c)
         drain(EARLY, c)
     for l in range(EARLY):
         for zt in range(blocks):
-            target[l + 1, zt, TOP : TOP + rows, :] += done[l + 1, zt, 16 : 16 + rows, :]
-            target[l + 1, zt, LOW : LOW + 1, :] += done[l + 1, zt, 15:16, :]
-            target[l + 1, zt, TOP + rows : TOP + rows + 1, :] += done[l + 1, zt, 16 + rows : 17 + rows, :]
+            target[l + 1, zt, TOP : TOP + rows, :] += done[l + 1, zt, 12 : 12 + rows, :]
+            target[l + 1, zt, LOW : LOW + 1, :] += done[l + 1, zt, 11:12, :]
+            target[l + 1, zt, TOP + rows : TOP + rows + 1, :] += done[l + 1, zt, 12 + rows : 13 + rows, :]
 
     last = SUBSTEPS - 1
     advance(nxt, None, 0)

time: 56.8 us -> 56.8 us (level)
  no operation moved by 1% of the time
where the time goes in v6:
time: 56.8 us; the launch traced here: 56.6 us
  Pallas kernels  55.3 us (97%)
  between operations  1.29 us (2%)
    pallas_call x1, Pallas kernels, call_step(): pl.pallas_call(functools.partial(step_kernel, fluids, subs), out_shape=(p...  53.2 us
    pallas_call x1, Pallas kernels, call_finish(): pl.pallas_call(finish_kernel, out_shape=tuple((jax.ShapeDtypeStruct(x.sha...  2.09 us

profile of v6, /device:TPU:1, one launch (start us, length us, event | category | flops | bytes accessed | tf_op | source)
XLA Modules:
  0.0 56.6 jit_solution(11940147980460978857)
XLA Ops:
  1.3 53.2 %step.1 = (f32[16,128]{1,0:T(8,128)S(1)}, f32[32,16,2048]{2,1,0:T(8,128)S(1)}, f32[16,128]{1,0:T(8,128)S(1)}) custom-call(s32[1]{0:T(128)S(6)} %copy.13.count, s32[2,256]{1,0:T(2,128)} %bitcast.13, f32[3,2048]{1,0:T(4,128)} %pos_in.1, f32[16,128]{1,0:T(8,128)} %bitcast.8, s32[16,128]{1,0:T(8,128)} %bitcast.9, s32[16,128]{1,0:T(8,128)} %bitcast.10, ...), custom_call_target="tpu_custom_call" | custom-call | tf_op jit(solution)/shard_map/step/pallas_call | solution.py:515
  54.5 2.1 %finish.1 = (f32[32,16,2048]{2,1,0:T(8,128)}, f32[16,128]{1,0:T(8,128)}, f32[16,128]{1,0:T(8,128)}) custom-call(f32[32,16,2048]{2,1,0:T(8,128)S(1)} %get-tuple-element.9.plate, f32[16,128]{1,0:T(8,128)S(1)} %get-tuple-element.10.first, f32[16,128]{1,0:T(8,128)S(1)} %get-tuple-element.11.second), custom_call_target="tpu_custom_call" | custom-call | tf_op jit(solution)/shard_map/finish/pallas_call | solution.py:592
